TPU v7x, 32 devices: a whole 2x2x4 slice. The times are simulated.
32 devices in a mesh: con: 4 (over x, core), res: 8 (over z, y).
Axes of the slice: x: 2, y: 2, z: 4, core: 2. Of those that a mesh axis runs over, the one named last changes fastest.
Arguments:
- integrals: float32 [24576, 24576], P('res', 'con'), as said below
- tile_mask: int32 [96, 96], P('res', 'con'), may hold values from 0 to 1, as said below
- amplitudes: float32 [24576, 384], P(('con', 'res')), may hold values from -4 to 4
- other_first: float32 [24576, 384], P(('res', 'con')), may hold values from -6 to 6
- other_second: float32 [24576, 384], P(('con', 'res')), may hold values from -6 to 6
- vir_index: int32 [2, 24576], replicated, may hold values from 0 to 1599
- occ_index: int32 [2, 384], replicated, may hold values from 0 to 31, as said below
- partner: int32 [384], replicated, may hold values from 0 to 383, as said below
- eps_vir: float32 [1600], replicated, may hold values from 0.2 to 3
- eps_occ: float32 [32], replicated, may hold values from -2 to -0.2
Outputs:
- first_update: float32 [24576, 384], P(('res', 'con'))
- second_update: float32 [24576, 384], P(('con', 'res'))
Inputs may be any that keep to these rules, and one draw needn't show every extreme that they name: integrals is symmetric: integrals[p, s] == integrals[s, p]. tile_mask is symmetric and its diagonal is 1. partner is a permutation that is its own inverse with no fixed point. The two orbitals of an occupied pair differ, and occ_index[0, partner[q]] == occ_index[1, q].
All inputs are finite; a program needn't handle non-finite values.
Results may differ from a plain program's by a relative error of at most 0.000065.
Values sent between devices are 32-bit elements; how exact they have to be, the bound alone decides.
No kernel may reach another device: no remote copies, remote signals or barrier semaphores. Data moves between devices by JAX's collectives and lax.ppermute only.
A program may use at most 320 MiB of HBM per device.

v0:
```python
import functools

import jax
import jax.numpy as jnp
from jax import lax
from jax.experimental import pallas as pl
from jax.experimental.pallas import tpu as pltpu
from jax.sharding import PartitionSpec as P


W = 256
PARTS = 2
DEPTH = 12
UNROLL = 4


f32 = jnp.float32
bf16 = jnp.bfloat16
precise = lax.Precision.HIGHEST


def pair_energy(pair_index, table):
    orbitals = lax.broadcasted_iota(jnp.int32, (1, table.shape[0]), 1)
    counts = (pair_index[0][:, None] == orbitals).astype(f32) + (pair_index[1][:, None] == orbitals).astype(f32)
    return jnp.dot(counts, table, precision=precise, preferred_element_type=f32)


def renew(ladder, other, vir_rows, occ_energy, swap_matrix):
    unscaled = (other + ladder) / (vir_rows[:, None] - occ_energy[None, :])
    swapped = jnp.dot(unscaled, swap_matrix, precision=precise, preferred_element_type=f32)
    return 0.5 * (unscaled - swapped)


def general(
    integrals, tile_mask, amplitudes, other_first, other_second, vir_index, occ_index, partner, eps_vir, eps_occ
):
    row_count, col_count = integrals.shape
    tiles_down, tiles_across = tile_mask.shape
    weights = tile_mask.astype(f32)
    screened = (integrals.reshape(tiles_down, W, tiles_across, W) * weights[:, None, :, None]).reshape(
        row_count, col_count
    )
    occ_energy = pair_energy(occ_index, eps_occ)
    occ_cols = amplitudes.shape[1]
    column_ids = lax.broadcasted_iota(jnp.int32, (occ_cols, occ_cols), 0)
    swap_matrix = (column_ids == partner[None, :]).astype(f32)
    n_con = lax.axis_size("con")
    n_res = lax.axis_size("res")
    con_at = lax.axis_index("con")
    res_at = lax.axis_index("res")
    fine_rows = amplitudes.shape[0]

    def vir_rows(offset):
        return pair_energy(lax.dynamic_slice_in_dim(vir_index, offset, fine_rows, 1), eps_vir)

    partial_one = jnp.dot(
        screened,
        lax.all_gather(amplitudes, "res", axis=0, tiled=True),
        precision=precise,
        preferred_element_type=f32,
    )
    ladder_one = lax.psum_scatter(partial_one, "con", scatter_dimension=0, tiled=True)
    first_vir = vir_rows((res_at * n_con + con_at) * fine_rows)
    first_update = renew(ladder_one, other_first, first_vir, occ_energy, swap_matrix)
    partial_two = lax.dot_general(
        screened,
        lax.all_gather(first_update, "con", axis=0, tiled=True),
        (((0,), (0,)), ((), ())),
        precision=precise,
        preferred_element_type=f32,
    )
    ladder_two = lax.psum_scatter(partial_two, "res", scatter_dimension=0, tiled=True)
    second_vir = vir_rows((con_at * n_res + res_at) * fine_rows)
    second_update = renew(ladder_two, other_second, second_vir, occ_energy, swap_matrix)
    return (first_update, second_update)


def halves(value):
    high = value.astype(bf16)
    return high, (value - high.astype(f32)).astype(bf16)


def sweep_kernel(by_rows, blocks, n_parts, has_start, n_out, strip_base, edge, starts, row_of, col_of, strip_of, place_of, a_hbm, *refs):
    n_x = len(blocks) * n_parts
    x_refs = refs[:n_x]
    start_ref = refs[n_x] if has_start else None
    refs = refs[n_x + has_start :]
    out_refs, refs = refs[:n_out], refs[n_out:]
    y_ref = out_refs[0] if n_out == 1 else refs[0]
    refs = refs if n_out == 1 else refs[1:]
    x_split, tiles, sems, x_sem = refs[:4]
    x_whole = refs[4:]
    first = starts[edge[0]]
    count = starts[edge[1]] - first

    def fetch(i):
        entry = first + i
        rows = pl.ds(pl.multiple_of(row_of[entry] * W, W), W)
        cols = pl.ds(pl.multiple_of(col_of[entry] * W, W), W)
        slot = lax.rem(i, DEPTH)
        return pltpu.make_async_copy(a_hbm.at[rows, cols], tiles.at[slot], sems.at[slot])

    part_rows = y_ref.shape[0] // n_parts
    loads = []
    for n in range(n_x):
        part = pl.ds((n % n_parts) * part_rows, part_rows)
        loads.append(pltpu.make_async_copy(x_refs[n], x_whole[n // n_parts].at[part, :], x_sem.at[n]))
        loads[-1].start()
    for i in range(DEPTH):

        @pl.when(i < count)
        def _():
            fetch(i).start()

    y_ref[...] = start_ref[...] if has_start else jnp.zeros_like(y_ref)
    width = y_ref.shape[0]
    at = 0
    for n in range(len(blocks)):
        for p in range(n_parts):
            loads[n * n_parts + p].wait()
        for j in range(blocks[n] // W):
            high, low = halves(x_whole[n][:, j * W : (j + 1) * W])
            x_split[at, :width, :] = high
            x_split[at, width:, :] = low
            at += 1

    def product(i):
        entry = first + i
        high, low = halves(tiles[lax.rem(i, DEPTH)])
        strip = strip_of[entry] - strip_base
        place = place_of[entry]
        source, target = (strip, place) if by_rows else (place, strip)
        dims = (((1,), (1 if by_rows else 0,)), ((), ()))
        both = x_split[source]
        main = lax.dot_general(both, high, dims, preferred_element_type=f32)
        rest = lax.dot_general(both[:width], low, dims, preferred_element_type=f32)
        return (main[:width] + main[width:]) + rest, pl.ds(pl.multiple_of(target * W, W), W)

    def several(block, _):
        at = block * UNROLL
        for u in range(UNROLL):
            fetch(at + u).wait()
        done = [product(at + u) for u in range(UNROLL)]
        for value, where in done:
            y_ref[:, where] += value
        for u in range(UNROLL):

            @pl.when(at + u + DEPTH < count)
            def _():
                fetch(at + u + DEPTH).start()

        return 0

    def single(i, _):
        fetch(i).wait()
        value, where = product(i)
        y_ref[:, where] += value
        return 0

    several_of = count // UNROLL
    lax.fori_loop(0, several_of, several, 0)
    lax.fori_loop(several_of * UNROLL, count, single, 0)
    if n_out > 1:
        out_cols = out_refs[0].shape[1]
        for n, out_ref in enumerate(out_refs):
            p, c = n % n_parts, n // n_parts
            out_ref[...] = y_ref[p * part_rows : (p + 1) * part_rows, c * out_cols : (c + 1) * out_cols]


def sweep(by_rows, tables, starts, edge, strip_tiles, integrals, x_blocks, y_width, start=None, pieces=0):
    n_parts = len(x_blocks[0])
    part_rows = x_blocks[0][0].shape[0]
    width = n_parts * part_rows
    blocks = [block[0].shape[1] for block in x_blocks]
    inputs = [part for block in x_blocks for part in block]
    scalar = pl.BlockSpec(memory_space=pltpu.SMEM)
    vector = pl.BlockSpec(memory_space=pltpu.VMEM)
    anywhere = pl.BlockSpec(memory_space=pl.ANY)
    has_start = start is not None
    n_out = pieces * n_parts if pieces else 1
    whole = jax.ShapeDtypeStruct((width, y_width), f32)
    tile_guess = (edge[1] - edge[0]) * strip_tiles * (integrals.shape[0] // W) // 2
    extra = [pltpu.VMEM((width, y_width), f32)] if pieces else []
    return pl.pallas_call(
        functools.partial(
            sweep_kernel, by_rows, blocks, n_parts, int(has_start), n_out, edge[0] * strip_tiles, edge
        ),
        out_shape=[jax.ShapeDtypeStruct((part_rows, y_width // pieces), f32)] * n_out if pieces else whole,
        in_specs=[scalar] * 5 + [anywhere] * (1 + len(inputs)) + [vector] * has_start,
        out_specs=[vector] * n_out if pieces else vector,
        scratch_shapes=extra
        + [
            pltpu.VMEM((sum(blocks) // W, 2 * width, W), bf16),
            pltpu.VMEM((DEPTH, W, W), f32),
            pltpu.SemaphoreType.DMA((DEPTH,)),
            pltpu.SemaphoreType.DMA((len(inputs),)),
        ]
        + [pltpu.VMEM((width, n), f32) for n in blocks],
        input_output_aliases={6 + len(inputs): 0} if has_start and not pieces else {},
        compiler_params=pltpu.CompilerParams(vmem_limit_bytes=32 * 2**20),
        cost_estimate=pl.CostEstimate(
            flops=6 * width * W * W * tile_guess, bytes_accessed=4 * W * W * tile_guess, transcendentals=0
        ),
        name="rows_sweep" if by_rows else "cols_sweep",
    )(starts, *tables, integrals, *inputs, *([start] if has_start else []))


def ring_order(n):
    return list(range(0, n, 2)) + list(range(n - 1, 0, -2))


def bit_reverse(value, bits):
    out = jnp.zeros_like(value)
    for b in range(bits):
        out = out + ((value >> b) & 1) * (1 << (bits - 1 - b))
    return out


def tile_tables(tile_mask, order, res_at, con_at, n_con, strip_tiles):
    down, across = tile_mask.shape
    n = len(order)
    ring = jnp.array(order, jnp.int32)
    my_place = jnp.sum(jnp.where(ring == res_at, jnp.arange(n, dtype=jnp.int32), 0))
    steps = [0]
    for s in range(1, n // 2):
        steps += [-s, s]
    steps.append(n // 2)
    places = lax.rem(my_place + jnp.array(steps, jnp.int32) + n, n)
    owners = jnp.sum(jnp.where(places[:, None] == jnp.arange(n, dtype=jnp.int32)[None, :], ring[None, :], 0), axis=1)
    cols = (owners[:, None] * strip_tiles + jnp.arange(strip_tiles, dtype=jnp.int32)[None, :]).reshape(across)
    chosen = (cols[:, None] == jnp.arange(across, dtype=jnp.int32)[None, :]).astype(f32)
    kept = lax.dot_general(chosen, (tile_mask != 0).astype(f32), (((1,), (1,)), ((), ())), preferred_element_type=f32)
    flags = kept.reshape(across * down).astype(jnp.int32)
    total = across * down
    entry = jnp.arange(total, dtype=jnp.int32)
    before = jnp.sum(jnp.where(entry[None, :] < entry[:, None], flags[None, :], 0), axis=1)
    slot = jnp.where(flags > 0, before, total)
    listed = jnp.sum(jnp.where(slot[None, :] == entry[:, None], entry[None, :], 0), axis=1)
    strip = listed // down
    row = listed - strip * down
    col = jnp.sum(jnp.where(strip[:, None] == jnp.arange(across, dtype=jnp.int32)[None, :], cols[None, :], 0), axis=1)
    bits = n_con.bit_length() - 1
    piece = row // strip_tiles
    place = bit_reverse(piece ^ con_at, bits) * strip_tiles + (row - piece * strip_tiles)
    edges = jnp.arange(n + 1, dtype=jnp.int32) * (strip_tiles * down)
    starts = jnp.sum(jnp.where(entry[None, :] < edges[:, None], flags[None, :], 0), axis=1)
    return (row, col, strip, place), starts


def vir_energies(vir_index, eps_vir, offset, count):
    picked = lax.dynamic_slice_in_dim(vir_index, offset, count, 1)
    orbitals = lax.broadcasted_iota(jnp.int32, (eps_vir.shape[0], 1), 0)
    table = eps_vir[:, None]
    first = jnp.sum(jnp.where(picked[0][None, :] == orbitals, table, 0.0), axis=0)
    second = jnp.sum(jnp.where(picked[1][None, :] == orbitals, table, 0.0), axis=0)
    return first + second


def tiled(
    integrals, tile_mask, amplitudes, other_first, other_second, vir_index, occ_index, partner, eps_vir, eps_occ
):
    n_con = lax.axis_size("con")
    n_res = lax.axis_size("res")
    con_at = lax.axis_index("con")
    res_at = lax.axis_index("res")
    fine, occ_cols = amplitudes.shape
    rows, _ = integrals.shape
    strip_tiles = fine // W
    pairs = occ_cols // 2
    width = pairs // PARTS
    parts = range(PARTS)

    column = jnp.arange(occ_cols, dtype=jnp.int32)
    lead = column < partner
    low = jnp.minimum(column, partner)
    pair_of = jnp.sum(jnp.where(column[None, :] < low[:, None], lead[None, :].astype(jnp.int32), 0), axis=1)
    is_pair = jnp.arange(pairs, dtype=jnp.int32)[:, None] == pair_of[None, :]
    chosen = (is_pair & lead[None, :]).astype(f32)
    signed = jnp.where(is_pair, jnp.where(lead, 1.0, -1.0)[None, :], 0.0).astype(f32)

    def compact(value):
        return lax.dot_general(
            signed, value, (((1,), (1,)), ((), ())), precision=precise, preferred_element_type=f32
        )

    def expand(value):
        return lax.dot_general(
            value, signed, (((0,), (0,)), ((), ())), precision=precise, preferred_element_type=f32
        )

    occ_orbitals = lax.broadcasted_iota(jnp.int32, (eps_occ.shape[0], 1), 0)
    occ_energy = jnp.sum(jnp.where(occ_index[0][None, :] == occ_orbitals, eps_occ[:, None], 0.0), axis=0) + jnp.sum(
        jnp.where(occ_index[1][None, :] == occ_orbitals, eps_occ[:, None], 0.0), axis=0
    )
    occ_pair = jnp.sum(chosen * occ_energy[None, :], axis=1)
    order = ring_order(n_res)
    onward = [(order[i], order[(i + 1) % n_res]) for i in range(n_res)]
    backward = [(b, a) for a, b in onward]
    tables, starts = tile_tables(tile_mask, order, res_at, con_at, n_con, strip_tiles)
    rows_sweep = functools.partial(sweep, True, tables, starts)
    cols_sweep = functools.partial(sweep, False, tables, starts)

    def cut(value):
        return [value[p * width : (p + 1) * width] for p in parts]

    def send(values, axis, perm):
        return [lax.ppermute(value, axis, perm) for value in values]

    def scales(index, offset):
        return cut(vir_energies(index, eps_vir, offset, fine)[None, :] - occ_pair[:, None])

    near = n_res // 2
    own = cut(compact(amplitudes))
    ahead = behind = own
    blocks = [own]
    ladder = None
    for s in range(1, near):
        ahead, behind = send(ahead, "res", onward), send(behind, "res", backward)
        blocks += [ahead, behind]
        edge = (2 * s + 1 - len(blocks), 2 * s + 1)
        ladder = rows_sweep(edge, strip_tiles, integrals, blocks, rows, ladder)
        blocks = []
    far = send(ahead[: PARTS // 2], "res", onward) + send(behind[PARTS // 2 :], "res", backward)
    pieces = rows_sweep((n_res - 1, n_res), strip_tiles, integrals, [far], rows, ladder, pieces=2)
    kept, sent = pieces[:PARTS], pieces[PARTS:]
    first_other = compact(other_first)
    bit = 1
    while bit < n_con:
        swap = [(i, i ^ bit) for i in range(n_con)]
        came = send(sent, "con", swap)
        bit *= 2
        if bit < n_con:
            mid = kept[0].shape[1] // 2
            sent = [kept[p][:, mid:] + came[p][:, mid:] for p in parts]
            kept = [kept[p][:, :mid] + came[p][:, :mid] for p in parts]
            late_index, sent[0] = lax.optimization_barrier((vir_index, sent[0]))
    first_scale = scales(late_index, (res_at * n_con + con_at) * fine)
    firsts = [0.5 * (part + (kept[p] + came[p])) / first_scale[p] for p, part in enumerate(cut(first_other))]
    held = [firsts]
    while bit > 1:
        bit //= 2
        swap = [(i, i ^ bit) for i in range(n_con)]
        block = [jnp.concatenate([h[p] for h in held], axis=1) if len(held) > 1 else held[0][p] for p in parts]
        held = held + [send(block, "con", swap)]
    far = cols_sweep((n_res - 1, n_res), strip_tiles, integrals, held, fine, pieces=1)
    ahead = [lax.ppermute(far[p], "res", onward) if p < PARTS // 2 else None for p in parts]
    behind = [None if p < PARTS // 2 else lax.ppermute(far[p], "res", backward) for p in parts]
    late_index, second_other_rows, _ = lax.optimization_barrier((vir_index, other_second, far[0]))
    for s in range(near - 1, 0, -1):
        edge = (2 * s - 1, 2 * s + 1)
        both = cols_sweep(edge, strip_tiles, integrals, held, 2 * fine, pieces=2)
        to_behind, to_ahead = both[:PARTS], both[PARTS:]
        ahead = send([to_ahead[p] if ahead[p] is None else to_ahead[p] + ahead[p] for p in parts], "res", onward)
        behind = send([to_behind[p] if behind[p] is None else to_behind[p] + behind[p] for p in parts], "res", backward)
    mine = cols_sweep((0, 1), strip_tiles, integrals, held, fine, pieces=1)
    second_other = cut(compact(second_other_rows))
    second_scale = scales(late_index, (con_at * n_res + res_at) * fine)
    seconds = [
        (0.5 * second_other[p] + ((mine[p] + ahead[p]) + behind[p])) / second_scale[p] for p in parts
    ]
    return expand(jnp.concatenate(firsts, axis=0)), expand(jnp.concatenate(seconds, axis=0))


def per_device(integrals, tile_mask, amplitudes, *rest):
    n_con = lax.axis_size("con")
    n_res = lax.axis_size("res")
    fits = (
        amplitudes.shape[0] % W == 0
        and amplitudes.shape[1] % (32 * PARTS) == 0
        and n_con & (n_con - 1) == 0
        and n_res % 2 == 0
        and n_res > 2
    )
    if not fits:
        return general(integrals, tile_mask, amplitudes, *rest)
    return tiled(integrals, tile_mask, amplitudes, *rest)


def solution(mesh):
    return jax.shard_map(
        per_device,
        mesh=mesh,
        in_specs=(
            P("res", "con"),
            P("res", "con"),
            P(("con", "res"), None),
            P(("res", "con"), None),
            P(("con", "res"), None),
            P(),
            P(),
            P(),
            P(),
            P(),
        ),
        out_specs=(P(("res", "con"), None), P(("con", "res"), None)),
        check_vma=False,
    )
```

profile of v0, /device:TPU:0, one launch (start us, length us, event | category | flops | bytes accessed | tf_op | source)
XLA Modules:
  0.0 172.2 jit_solution(2588882017789812355)
XLA Ops:
  3.9 3.1 %collective-permute-start = (f32[96,768]{1,0:T(8,128)S(1)}, f32[96,768]{1,0:T(8,128)S(1)}, u32[]{:S(2)}, u32[]{:S(2)}) collective-permute-start(f32[96,768]{1,0:T(8,128)S(1)} %get-tuple-element.71.refs_0_), channel_id=1, source_target_pairs={{0,2},{2,4},{4,6},{6,7},{7,5},{5,3},{3,1},{1,0},{8,10},{10,12},{12... | collective-permute-start | bytes 884744 | tf_op jit(solution)/shard_map/ppermute | solution.py:307
  11.5 3.3 %collective-permute-done.refs_2_ = f32[96,768]{1,0:T(8,128)S(1)} collective-permute-done((f32[96,768]{1,0:T(8,128)S(1)}, f32[96,768]{1,0:T(8,128)S(1)}, u32[]{:S(2)}, u32[]{:S(2)}) %collective-permute-start) | collective-permute-done | bytes 294944 | tf_op jit(solution)/shard_map/ppermute | solution.py:307
  14.8 2.1 %collective-permute-start.1 = (f32[96,768]{1,0:T(8,128)S(1)}, f32[96,768]{1,0:T(8,128)S(1)}, u32[]{:S(2)}, u32[]{:S(2)}) collective-permute-start(f32[96,768]{1,0:T(8,128)S(1)} %collective-permute-done.refs_2_), channel_id=1, source_target_pairs={{0,2},{2,4},{4,6},{6,7},{7,5},{5,3},{3,1},{1,0},{8,10},{10,12},{12... | collective-permute-start | bytes 884744 | tf_op jit(solution)/shard_map/ppermute | solution.py:307
  16.9 6.3 %collective-permute-done.4.refs_5_ = f32[96,768]{1,0:T(8,128)S(1)} collective-permute-done((f32[96,768]{1,0:T(8,128)S(1)}, f32[96,768]{1,0:T(8,128)S(1)}, u32[]{:S(2)}, u32[]{:S(2)}) %collective-permute-start.4) | collective-permute-done | bytes 294944 | tf_op jit(solution)/shard_map/ppermute | solution.py:307
  27.4 2.1 %collective-permute-start.2 = (f32[96,768]{1,0:T(8,128)S(1)}, f32[96,768]{1,0:T(8,128)S(1)}, u32[]{:S(2)}, u32[]{:S(2)}) collective-permute-start(f32[96,768]{1,0:T(8,128)S(1)} %collective-permute-done.1.refs_0_), channel_id=1, source_target_pairs={{0,2},{2,4},{4,6},{6,7},{7,5},{5,3},{3,1},{1,0},{8,10},{10,12},{12... | collective-permute-start | bytes 884744 | tf_op jit(solution)/shard_map/ppermute | solution.py:307
  29.5 4.9 %collective-permute-done.5.refs_3_ = f32[96,768]{1,0:T(8,128)S(1)} collective-permute-done((f32[96,768]{1,0:T(8,128)S(1)}, f32[96,768]{1,0:T(8,128)S(1)}, u32[]{:S(2)}, u32[]{:S(2)}) %collective-permute-start.5) | collective-permute-done | bytes 294944 | tf_op jit(solution)/shard_map/ppermute | solution.py:307
  36.7 12.7 %rows_sweep.4.refs_4_ = f32[192,3072]{1,0:T(8,128)S(1)} custom-call(s32[9]{0:T(128)S(1)} %select_reduce_fusion.11.starts, s32[288]{0:T(512)S(1)} %get-tuple-element.65.row_of, s32[288]{0:T(512)S(1)} %select_reduce_fusion.10.col_of, s32[288]{0:T(512)S(1)} %get-tuple-element.72.strip_of, s32[288]{0:T(512)S(1)} %get-tuple-element.64.place_of, ...), custom_call_target="tpu_custom_call" | custom-call | flops 4076863488 | bytes 14155776 | tf_op jit(solution)/shard_map/rows_sweep/pallas_call | solution.py:184
  51.6 9.0 %rows_sweep.5.refs_4_ = f32[192,3072]{1,0:T(8,128)S(1)} custom-call(s32[9]{0:T(128)S(1)} %select_reduce_fusion.11.starts, s32[288]{0:T(512)S(1)} %get-tuple-element.65.row_of, s32[288]{0:T(512)S(1)} %select_reduce_fusion.10.col_of, s32[288]{0:T(512)S(1)} %get-tuple-element.72.strip_of, ...), custom_call_target="tpu_custom_call", output_to_operand_aliasing={{}: (10, {})} | custom-call | flops 2717908992 | bytes 9437184 | tf_op jit(solution)/shard_map/rows_sweep/pallas_call | solution.py:184
  60.7 8.1 %rows_sweep.6.refs_2_ = f32[192,3072]{1,0:T(8,128)S(1)} custom-call(s32[9]{0:T(128)S(1)} %select_reduce_fusion.11.starts, s32[288]{0:T(512)S(1)} %get-tuple-element.65.row_of, s32[288]{0:T(512)S(1)} %select_reduce_fusion.10.col_of, s32[288]{0:T(512)S(1)} %get-tuple-element.72.strip_of, ...), custom_call_target="tpu_custom_call", output_to_operand_aliasing={{}: (10, {})} | custom-call | flops 2717908992 | bytes 9437184 | tf_op jit(solution)/shard_map/rows_sweep/pallas_call | solution.py:184
  68.9 5.2 %rows_sweep.7 = (f32[96,1536]{1,0:T(8,128)S(1)}, f32[96,1536]{1,0:T(8,128)S(1)}, f32[96,1536]{1,0:T(8,128)S(1)}, f32[96,1536]{1,0:T(8,128)S(1)}) custom-call(s32[9]{0:T(128)S(1)} %select_reduce_fusion.11.starts, s32[288]{0:T(512)S(1)} %get-tuple-element.65.row_of, s32[288]{0:T(512)S(1)} %select_reduce_fusion.10.col_of, s32[288]{0:T(512)S(1)} %get-tuple-element.72.strip_of, ...), custom_call_target="tpu_custom_call" | custom-call | flops 1358954496 | bytes 4718592 | tf_op jit(solution)/shard_map/rows_sweep/pallas_call | solution.py:184
  80.8 5.6 %collective-permute-done.17 = f32[96,768]{1,0:T(8,128)S(1)} collective-permute-done((f32[96,768]{1,0:T(8,128)S(1)}, f32[96,768]{1,0:T(8,128)S(1)}, u32[]{:S(2)}, u32[]{:S(2)}) %collective-permute-start.17) | collective-permute-done | bytes 294944 | tf_op jit(solution)/shard_map/ppermute | solution.py:307
  86.4 5.4 %collective-permute-done.15 = f32[96,768]{1,0:T(8,128)S(1)} collective-permute-done((f32[96,768]{1,0:T(8,128)S(1)}, f32[96,768]{1,0:T(8,128)S(1)}, u32[]{:S(2)}, u32[]{:S(2)}) %collective-permute-start.15) | collective-permute-done | bytes 294944 | tf_op jit(solution)/shard_map/ppermute | solution.py:307
  94.1 7.9 %collective-permute-done.19.refs_3_ = f32[96,768]{1,0:T(8,128)S(1)} collective-permute-done((f32[96,768]{1,0:T(8,128)S(1)}, f32[96,768]{1,0:T(8,128)S(1)}, u32[]{:S(2)}, u32[]{:S(2)}) %collective-permute-start.19) | collective-permute-done | bytes 294944 | tf_op jit(solution)/shard_map/ppermute | solution.py:307
  102.9 3.7 %collective-permute-done.18.refs_2_ = f32[96,768]{1,0:T(8,128)S(1)} collective-permute-done((f32[96,768]{1,0:T(8,128)S(1)}, f32[96,768]{1,0:T(8,128)S(1)}, u32[]{:S(2)}, u32[]{:S(2)}) %collective-permute-start.18) | collective-permute-done | bytes 294944 | tf_op jit(solution)/shard_map/ppermute | solution.py:307
  107.4 2.2 %collective-permute-done.20.refs_4_ = f32[96,1536]{1,0:T(8,128)S(1)} collective-permute-done((f32[96,1536]{1,0:T(8,128)}, f32[96,1536]{1,0:T(8,128)S(1)}, u32[]{:S(2)}, u32[]{:S(2)}) %collective-permute-start.20) | collective-permute-done | bytes 589856 | tf_op jit(solution)/shard_map/ppermute | solution.py:307
  110.3 4.8 %cols_sweep.5 = (f32[96,768]{1,0:T(8,128)S(1)}, f32[96,768]{1,0:T(8,128)S(1)}) custom-call(s32[9]{0:T(128)S(1)} %copy-done.2, s32[288]{0:T(512)S(1)} %get-tuple-element.65.row_of, s32[288]{0:T(512)S(1)} %select_reduce_fusion.10.col_of, s32[288]{0:T(512)S(1)} %get-tuple-element.72.strip_of, s32[288]{0:T(512)S(1)} %get-tuple-element.64.place_of, ...), custom_call_target="tpu_custom_call" | custom-call | flops 1358954496 | bytes 4718592 | tf_op jit(solution)/shard_map/cols_sweep/pallas_call | solution.py:184
  117.2 2.5 %fusion.4 = f32[768,384]{1,0:T(8,128)} fusion(f32[96,768]{1,0:T(8,128)S(1)} %get-tuple-element.69.refs_1_, f32[96,768]{1,0:T(8,128)S(1)} %get-tuple-element.68.refs_0_, f32[384]{0:T(512)S(1)} %copy-done.10, s32[384]{0:T(512)S(1)} %copy-done.7), kind=kOutput, calls=%fused_computation.13 | convolution fusion | flops 679772160 | bytes 1772544 | tf_op jit(solution)/shard_map/dot_general | solution.py:287
  119.7 7.7 %cols_sweep.9 = (f32[96,768]{1,0:T(8,128)S(1)}, f32[96,768]{1,0:T(8,128)S(1)}, f32[96,768]{1,0:T(8,128)S(1)}, f32[96,768]{1,0:T(8,128)S(1)}) custom-call(s32[9]{0:T(128)S(1)} %copy-done.2, s32[288]{0:T(512)S(1)} %get-tuple-element.65.row_of, s32[288]{0:T(512)S(1)} %select_reduce_fusion.10.col_of, s32[288]{0:T(512)S(1)} %get-tuple-element.72.strip_of, ...), custom_call_target="tpu_custom_call" | custom-call | flops 2717908992 | bytes 9437184 | tf_op jit(solution)/shard_map/cols_sweep/pallas_call | solution.py:184
  133.7 8.5 %cols_sweep.8 = (f32[96,768]{1,0:T(8,128)S(1)}, f32[96,768]{1,0:T(8,128)S(1)}, f32[96,768]{1,0:T(8,128)S(1)}, f32[96,768]{1,0:T(8,128)S(1)}) custom-call(s32[9]{0:T(128)S(1)} %copy-done.2, s32[288]{0:T(512)S(1)} %get-tuple-element.65.row_of, s32[288]{0:T(512)S(1)} %select_reduce_fusion.10.col_of, s32[288]{0:T(512)S(1)} %get-tuple-element.72.strip_of, ...), custom_call_target="tpu_custom_call" | custom-call | flops 2717908992 | bytes 9437184 | tf_op jit(solution)/shard_map/cols_sweep/pallas_call | solution.py:184
  142.4 2.1 %collective-permute-start.27 = (f32[96,768]{1,0:T(8,128)S(1)}, f32[96,768]{1,0:T(8,128)S(1)}, u32[]{:S(2)}, u32[]{:S(2)}) collective-permute-start(f32[96,768]{1,0:T(8,128)S(1)} %add.175), channel_id=1, source_target_pairs={{2,0},{4,2},{6,4},{7,6},{5,7},{3,5},{1,3},{0,1},{10,8},{12,10},{14... | collective-permute-start | bytes 884744 | tf_op jit(solution)/shard_map/ppermute | solution.py:307
  146.8 9.1 %cols_sweep.7 = (f32[96,768]{1,0:T(8,128)S(1)}, f32[96,768]{1,0:T(8,128)S(1)}, f32[96,768]{1,0:T(8,128)S(1)}, f32[96,768]{1,0:T(8,128)S(1)}) custom-call(s32[9]{0:T(128)S(1)} %copy-done.2, s32[288]{0:T(512)S(1)} %get-tuple-element.65.row_of, s32[288]{0:T(512)S(1)} %select_reduce_fusion.10.col_of, s32[288]{0:T(512)S(1)} %get-tuple-element.72.strip_of, ...), custom_call_target="tpu_custom_call" | custom-call | flops 2717908992 | bytes 9437184 | tf_op jit(solution)/shard_map/cols_sweep/pallas_call | solution.py:184
  160.4 4.9 %cols_sweep.6 = (f32[96,768]{1,0:T(8,128)S(1)}, f32[96,768]{1,0:T(8,128)S(1)}) custom-call(s32[9]{0:T(128)S(1)} %copy-done.2, s32[288]{0:T(512)S(1)} %get-tuple-element.65.row_of, s32[288]{0:T(512)S(1)} %select_reduce_fusion.10.col_of, s32[288]{0:T(512)S(1)} %get-tuple-element.72.strip_of, s32[288]{0:T(512)S(1)} %get-tuple-element.64.place_of, ...), custom_call_target="tpu_custom_call" | custom-call | flops 1358954496 | bytes 4718592 | tf_op jit(solution)/shard_map/cols_sweep/pallas_call | solution.py:184
  166.7 2.7 %collective-permute-done.35 = f32[96,768]{1,0:T(8,128)S(1)} collective-permute-done((f32[96,768]{1,0:T(8,128)S(1)}, f32[96,768]{1,0:T(8,128)S(1)}, u32[]{:S(2)}, u32[]{:S(2)}) %collective-permute-start.35) | collective-permute-done | bytes 294944 | tf_op jit(solution)/shard_map/ppermute | solution.py:307
  169.6 2.5 %fusion = f32[768,384]{1,0:T(8,128)} fusion(f32[96,768]{1,0:T(8,128)S(1)} %get-tuple-element.67, f32[96,768]{1,0:T(8,128)S(1)} %get-tuple-element.66, f32[384]{0:T(512)S(1)} %copy-done.10, s32[384]{0:T(512)S(1)} %copy-done.7), kind=kOutput, calls=%fused_computation.9 | convolution fusion | flops 679772160 | bytes 1772544 | tf_op jit(solution)/shard_map/dot_general | solution.py:287
  (155 shorter events, 44.5 us)
Async XLA Ops:
  7.0 16.2 %collective-permute-start.4 = (f32[96,768]{1,0:T(8,128)S(1)}, f32[96,768]{1,0:T(8,128)S(1)}, u32[]{:S(2)}, u32[]{:S(2)}) collective-permute-start(f32[96,768]{1,0:T(8,128)S(1)} %get-tuple-element.70.refs_1_), channel_id=1, source_target_pairs={{2,0},{4,2},{6,4},{7,6},{5,7},{3,5},{1,3},{0,1},{10,8},{12,10},{14... | collective-permute-start | bytes 884744 | tf_op jit(solution)/shard_map/ppermute | solution.py:307
  9.0 14.2 %collective-permute-start.8 = (f32[96,768]{1,0:T(8,128)S(1)}, f32[96,768]{1,0:T(8,128)S(1)}, u32[]{:S(2)}, u32[]{:S(2)}) collective-permute-start(f32[96,768]{1,0:T(8,128)S(1)} %get-tuple-element.70.refs_1_), channel_id=1, source_target_pairs={{0,2},{2,4},{4,6},{6,7},{7,5},{5,3},{3,1},{1,0},{8,10},{10,12},{12... | collective-permute-start | bytes 884744 | tf_op jit(solution)/shard_map/ppermute | solution.py:307
  14.8 12.6 %collective-permute-start.1 = (f32[96,768]{1,0:T(8,128)S(1)}, f32[96,768]{1,0:T(8,128)S(1)}, u32[]{:S(2)}, u32[]{:S(2)}) collective-permute-start(f32[96,768]{1,0:T(8,128)S(1)} %collective-permute-done.refs_2_), channel_id=1, source_target_pairs={{0,2},{2,4},{4,6},{6,7},{7,5},{5,3},{3,1},{1,0},{8,10},{10,12},{12... | collective-permute-start | bytes 884744 | tf_op jit(solution)/shard_map/ppermute | solution.py:307
  16.9 19.6 %collective-permute-start.12 = (f32[96,768]{1,0:T(8,128)S(1)}, f32[96,768]{1,0:T(8,128)S(1)}, u32[]{:S(2)}, u32[]{:S(2)}) collective-permute-start(f32[96,768]{1,0:T(8,128)S(1)} %collective-permute-done.11.refs_4_), channel_id=1, source_target_pairs={{2,0},{4,2},{6,4},{7,6},{5,7},{3,5},{1,3},{0,1},{10,8},{12,10},{14... | collective-permute-start | bytes 884744 | tf_op jit(solution)/shard_map/ppermute | solution.py:307
  23.2 11.5 %collective-permute-start.9 = (f32[96,768]{1,0:T(8,128)S(1)}, f32[96,768]{1,0:T(8,128)S(1)}, u32[]{:S(2)}, u32[]{:S(2)}) collective-permute-start(f32[96,768]{1,0:T(8,128)S(1)} %collective-permute-done.8.refs_3_), channel_id=1, source_target_pairs={{0,2},{2,4},{4,6},{6,7},{7,5},{5,3},{3,1},{1,0},{8,10},{10,12},{12... | collective-permute-start | bytes 884744 | tf_op jit(solution)/shard_map/ppermute | solution.py:307
  27.4 22.1 %collective-permute-start.2 = (f32[96,768]{1,0:T(8,128)S(1)}, f32[96,768]{1,0:T(8,128)S(1)}, u32[]{:S(2)}, u32[]{:S(2)}) collective-permute-start(f32[96,768]{1,0:T(8,128)S(1)} %collective-permute-done.1.refs_0_), channel_id=1, source_target_pairs={{0,2},{2,4},{4,6},{6,7},{7,5},{5,3},{3,1},{1,0},{8,10},{10,12},{12... | collective-permute-start | bytes 884744 | tf_op jit(solution)/shard_map/ppermute | solution.py:307
  34.4 15.2 %collective-permute-start.6 = (f32[96,768]{1,0:T(8,128)S(1)}, f32[96,768]{1,0:T(8,128)S(1)}, u32[]{:S(2)}, u32[]{:S(2)}) collective-permute-start(f32[96,768]{1,0:T(8,128)S(1)} %collective-permute-done.5.refs_3_), channel_id=1, source_target_pairs={{2,0},{4,2},{6,4},{7,6},{5,7},{3,5},{1,3},{0,1},{10,8},{12,10},{14... | collective-permute-start | bytes 884744 | tf_op jit(solution)/shard_map/ppermute | solution.py:307
  34.7 25.9 %collective-permute-start.10 = (f32[96,768]{1,0:T(8,128)S(1)}, f32[96,768]{1,0:T(8,128)S(1)}, u32[]{:S(2)}, u32[]{:S(2)}) collective-permute-start(f32[96,768]{1,0:T(8,128)S(1)} %collective-permute-done.9.refs_1_), channel_id=1, source_target_pairs={{0,2},{2,4},{4,6},{6,7},{7,5},{5,3},{3,1},{1,0},{8,10},{10,12},{12... | collective-permute-start | bytes 884744 | tf_op jit(solution)/shard_map/ppermute | solution.py:307
  36.5 24.2 %collective-permute-start.13 = (f32[96,768]{1,0:T(8,128)S(1)}, f32[96,768]{1,0:T(8,128)S(1)}, u32[]{:S(2)}, u32[]{:S(2)}) collective-permute-start(f32[96,768]{1,0:T(8,128)S(1)} %collective-permute-done.12.refs_2_), channel_id=1, source_target_pairs={{2,0},{4,2},{6,4},{7,6},{5,7},{3,5},{1,3},{0,1},{10,8},{12,10},{14... | collective-permute-start | bytes 884744 | tf_op jit(solution)/shard_map/ppermute | solution.py:307
  49.5 19.3 %collective-permute-start.3 = (f32[96,768]{1,0:T(8,128)S(1)}, f32[96,768]{1,0:T(8,128)S(1)}, u32[]{:S(2)}, u32[]{:S(2)}) collective-permute-start(f32[96,768]{1,0:T(8,128)S(1)} %collective-permute-done.2.refs_0_), channel_id=1, source_target_pairs={{0,2},{2,4},{4,6},{6,7},{7,5},{5,3},{3,1},{1,0},{8,10},{10,12},{12... | collective-permute-start | bytes 884744 | tf_op jit(solution)/shard_map/ppermute | solution.py:307
  49.6 19.3 %collective-permute-start.7 = (f32[96,768]{1,0:T(8,128)S(1)}, f32[96,768]{1,0:T(8,128)S(1)}, u32[]{:S(2)}, u32[]{:S(2)}) collective-permute-start(f32[96,768]{1,0:T(8,128)S(1)} %collective-permute-done.6.refs_3_), channel_id=1, source_target_pairs={{2,0},{4,2},{6,4},{7,6},{5,7},{3,5},{1,3},{0,1},{10,8},{12,10},{14... | collective-permute-start | bytes 884744 | tf_op jit(solution)/shard_map/ppermute | solution.py:307
  77.0 14.8 %collective-permute-start.15 = (f32[96,768]{1,0:T(8,128)S(1)}, f32[96,768]{1,0:T(8,128)S(1)}, u32[]{:S(2)}, u32[]{:S(2)}) collective-permute-start(f32[96,768]{1,0:T(8,128)S(1)} %slice_add_fusion.2), channel_id=1, source_target_pairs={{0,16},{8,24},{16,0},{24,8},{1,17},{9,25},{17,1},{25,9},{2,18},{10... | collective-permute-start | bytes 884744 | tf_op jit(solution)/shard_map/ppermute | solution.py:307
  92.4 14.1 %collective-permute-start.18 = (f32[96,768]{1,0:T(8,128)S(1)}, f32[96,768]{1,0:T(8,128)S(1)}, u32[]{:S(2)}, u32[]{:S(2)}) collective-permute-start(f32[96,768]{1,0:T(8,128)S(1)} %get-tuple-element.68.refs_0_), channel_id=1, source_target_pairs={{0,16},{8,24},{16,0},{24,8},{1,17},{9,25},{17,1},{25,9},{2,18},{10... | collective-permute-start | bytes 884744 | tf_op jit(solution)/shard_map/ppermute | solution.py:307
  115.1 15.2 %collective-permute-start.32 = (f32[96,768]{1,0:T(8,128)S(1)}, f32[96,768]{1,0:T(8,128)S(1)}, u32[]{:S(2)}, u32[]{:S(2)}) collective-permute-start(f32[96,768]{1,0:T(8,128)S(1)} %get-tuple-element.49), channel_id=1, source_target_pairs={{2,0},{4,2},{6,4},{7,6},{5,7},{3,5},{1,3},{0,1},{10,8},{12,10},{14... | collective-permute-start | bytes 884744 | tf_op jit(solution)/shard_map/ppermute | solution.py:347
  115.2 15.4 %collective-permute-start.22 = (f32[96,768]{1,0:T(8,128)S(1)}, f32[96,768]{1,0:T(8,128)S(1)}, u32[]{:S(2)}, u32[]{:S(2)}) collective-permute-start(f32[96,768]{1,0:T(8,128)S(1)} %get-tuple-element.32), channel_id=1, source_target_pairs={{0,2},{2,4},{4,6},{6,7},{7,5},{5,3},{3,1},{1,0},{8,10},{10,12},{12... | collective-permute-start | bytes 884744 | tf_op jit(solution)/shard_map/ppermute | solution.py:346
  127.4 14.8 %collective-permute-start.29 = (f32[96,768]{1,0:T(8,128)S(1)}, f32[96,768]{1,0:T(8,128)S(1)}, u32[]{:S(2)}, u32[]{:S(2)}) collective-permute-start(f32[96,768]{1,0:T(8,128)S(1)} %get-tuple-element.45), channel_id=1, source_target_pairs={{0,2},{2,4},{4,6},{6,7},{7,5},{5,3},{3,1},{1,0},{8,10},{10,12},{12... | collective-permute-start | bytes 884744 | tf_op jit(solution)/shard_map/ppermute | solution.py:307
  127.5 14.9 %collective-permute-start.26 = (f32[96,768]{1,0:T(8,128)S(1)}, f32[96,768]{1,0:T(8,128)S(1)}, u32[]{:S(2)}, u32[]{:S(2)}) collective-permute-start(f32[96,768]{1,0:T(8,128)S(1)} %get-tuple-element.40), channel_id=1, source_target_pairs={{2,0},{4,2},{6,4},{7,6},{5,7},{3,5},{1,3},{0,1},{10,8},{12,10},{14... | collective-permute-start | bytes 884744 | tf_op jit(solution)/shard_map/ppermute | solution.py:307
  130.4 14.1 %collective-permute-start.33 = (f32[96,768]{1,0:T(8,128)S(1)}, f32[96,768]{1,0:T(8,128)S(1)}, u32[]{:S(2)}, u32[]{:S(2)}) collective-permute-start(f32[96,768]{1,0:T(8,128)S(1)} %add.185), channel_id=1, source_target_pairs={{2,0},{4,2},{6,4},{7,6},{5,7},{3,5},{1,3},{0,1},{10,8},{12,10},{14... | collective-permute-start | bytes 884744 | tf_op jit(solution)/shard_map/ppermute | solution.py:307
  130.6 13.9 %collective-permute-start.23 = (f32[96,768]{1,0:T(8,128)S(1)}, f32[96,768]{1,0:T(8,128)S(1)}, u32[]{:S(2)}, u32[]{:S(2)}) collective-permute-start(f32[96,768]{1,0:T(8,128)S(1)} %add.171), channel_id=1, source_target_pairs={{0,2},{2,4},{4,6},{6,7},{7,5},{5,3},{3,1},{1,0},{8,10},{10,12},{12... | collective-permute-start | bytes 884744 | tf_op jit(solution)/shard_map/ppermute | solution.py:307
  142.3 13.6 %collective-permute-start.30 = (f32[96,768]{1,0:T(8,128)S(1)}, f32[96,768]{1,0:T(8,128)S(1)}, u32[]{:S(2)}, u32[]{:S(2)}) collective-permute-start(f32[96,768]{1,0:T(8,128)S(1)} %add.182), channel_id=1, source_target_pairs={{0,2},{2,4},{4,6},{6,7},{7,5},{5,3},{3,1},{1,0},{8,10},{10,12},{12... | collective-permute-start | bytes 884744 | tf_op jit(solution)/shard_map/ppermute | solution.py:307
  142.4 13.6 %collective-permute-start.27 = (f32[96,768]{1,0:T(8,128)S(1)}, f32[96,768]{1,0:T(8,128)S(1)}, u32[]{:S(2)}, u32[]{:S(2)}) collective-permute-start(f32[96,768]{1,0:T(8,128)S(1)} %add.175), channel_id=1, source_target_pairs={{2,0},{4,2},{6,4},{7,6},{5,7},{3,5},{1,3},{0,1},{10,8},{12,10},{14... | collective-permute-start | bytes 884744 | tf_op jit(solution)/shard_map/ppermute | solution.py:307
  144.5 13.7 %collective-permute-start.34 = (f32[96,768]{1,0:T(8,128)S(1)}, f32[96,768]{1,0:T(8,128)S(1)}, u32[]{:S(2)}, u32[]{:S(2)}) collective-permute-start(f32[96,768]{1,0:T(8,128)S(1)} %add.186), channel_id=1, source_target_pairs={{2,0},{4,2},{6,4},{7,6},{5,7},{3,5},{1,3},{0,1},{10,8},{12,10},{14... | collective-permute-start | bytes 884744 | tf_op jit(solution)/shard_map/ppermute | solution.py:307
  144.6 13.7 %collective-permute-start.24 = (f32[96,768]{1,0:T(8,128)S(1)}, f32[96,768]{1,0:T(8,128)S(1)}, u32[]{:S(2)}, u32[]{:S(2)}) collective-permute-start(f32[96,768]{1,0:T(8,128)S(1)} %add.172), channel_id=1, source_target_pairs={{0,2},{2,4},{4,6},{6,7},{7,5},{5,3},{3,1},{1,0},{8,10},{10,12},{12... | collective-permute-start | bytes 884744 | tf_op jit(solution)/shard_map/ppermute | solution.py:307
  158.2 11.2 %collective-permute-start.35 = (f32[96,768]{1,0:T(8,128)S(1)}, f32[96,768]{1,0:T(8,128)S(1)}, u32[]{:S(2)}, u32[]{:S(2)}) collective-permute-start(f32[96,768]{1,0:T(8,128)S(1)} %add.187), channel_id=1, source_target_pairs={{2,0},{4,2},{6,4},{7,6},{5,7},{3,5},{1,3},{0,1},{10,8},{12,10},{14... | collective-permute-start | bytes 884744 | tf_op jit(solution)/shard_map/ppermute | solution.py:307
  (34 other events, 278.3 us)
where the time goes:
time: 173 us; the launch traced here: 172 us
  Pallas kernels  70.1 us (41%)
  waiting for transfers between devices  44.4 us (26%)
  starting transfers between devices  35 us (20%)
  matrix products  9.51 us (5%)
  other arithmetic  9.14 us (5%)
  local copies, waits for them, and re-layouts  2.82 us (2%)
    pallas_call x9, Pallas kernels, sweep(): pl.pallas_call(functools.partial(sweep_kernel, by_rows, blocks, n_parts,...  70.1 us
    ppermute x34, waiting for transfers between devices, send(): return [lax.ppermute(value, axis, perm) for value in values]  44.4 us
    ppermute x34, starting transfers between devices, send(): return [lax.ppermute(value, axis, perm) for value in values]  32.9 us
    dot_general x2, matrix products, expand(): lax.dot_general(value, signed, (((0,), (0,)), ((), ())), precision=precis...  5.04 us
    dot_general x3, matrix products, compact(): lax.dot_general(signed, value, (((1,), (1,)), ((), ())), precision=precis...  4.28 us
  transfers between devices with their start and end apart: 36, of which 11 were waited for; matrix products, arithmetic and copies ran while one was open for 8% of the time, Pallas kernels for 35%

commit v1 on v0

--- a/solution.py
+++ b/solution.py
@@ -310,7 +310,7 @@
         return cut(vir_energies(index, eps_vir, offset, fine)[None, :] - occ_pair[:, None])
 
     near = n_res // 2
-    own = cut(compact(amplitudes))
+    own = [compact(amplitudes)]
     ahead = behind = own
     blocks = [own]
     ladder = None
@@ -320,7 +320,8 @@
         edge = (2 * s + 1 - len(blocks), 2 * s + 1)
         ladder = rows_sweep(edge, strip_tiles, integrals, blocks, rows, ladder)
         blocks = []
-    far = send(ahead[: PARTS // 2], "res", onward) + send(behind[PARTS // 2 :], "res", backward)
+    far = send(cut(ahead[0])[: PARTS // 2], "res", onward)
+    far += send(cut(behind[0])[PARTS // 2 :], "res", backward)
     pieces = rows_sweep((n_res - 1, n_res), strip_tiles, integrals, [far], rows, ladder, pieces=2)
     kept, sent = pieces[:PARTS], pieces[PARTS:]
     first_other = compact(other_first)
@@ -333,19 +334,28 @@
             mid = kept[0].shape[1] // 2
             sent = [kept[p][:, mid:] + came[p][:, mid:] for p in parts]
             kept = [kept[p][:, :mid] + came[p][:, :mid] for p in parts]
-            late_index, sent[0] = lax.optimization_barrier((vir_index, sent[0]))
-    first_scale = scales(late_index, (res_at * n_con + con_at) * fine)
-    firsts = [0.5 * (part + (kept[p] + came[p])) / first_scale[p] for p, part in enumerate(cut(first_other))]
+            late_index, late_other, sent[0] = lax.optimization_barrier((vir_index, other_second, sent[0]))
+    ready = (
+        scales(late_index, (res_at * n_con + con_at) * fine),
+        scales(late_index, (con_at * n_res + res_at) * fine),
+        cut(compact(late_other)),
+    )
+    first_scale, second_scale, second_other = lax.optimization_barrier(ready)
+    firsts = []
+    for p, part in enumerate(cut(first_other)):
+        if firsts:
+            came[p], firsts[-1] = lax.optimization_barrier((came[p], firsts[-1]))
+        firsts.append(0.5 * (part + (kept[p] + came[p])) / first_scale[p])
     held = [firsts]
     while bit > 1:
         bit //= 2
         swap = [(i, i ^ bit) for i in range(n_con)]
         block = [jnp.concatenate([h[p] for h in held], axis=1) if len(held) > 1 else held[0][p] for p in parts]
-        held = held + [send(block, "con", swap)]
+        held = held + [send(block[:-1], "con", swap) + send(block[-1:], "con", swap)]
+    first_out = expand(jnp.concatenate(firsts, axis=0))
     far = cols_sweep((n_res - 1, n_res), strip_tiles, integrals, held, fine, pieces=1)
     ahead = [lax.ppermute(far[p], "res", onward) if p < PARTS // 2 else None for p in parts]
     behind = [None if p < PARTS // 2 else lax.ppermute(far[p], "res", backward) for p in parts]
-    late_index, second_other_rows, _ = lax.optimization_barrier((vir_index, other_second, far[0]))
     for s in range(near - 1, 0, -1):
         edge = (2 * s - 1, 2 * s + 1)
         both = cols_sweep(edge, strip_tiles, integrals, held, 2 * fine, pieces=2)
@@ -353,12 +363,10 @@
         ahead = send([to_ahead[p] if ahead[p] is None else to_ahead[p] + ahead[p] for p in parts], "res", onward)
         behind = send([to_behind[p] if behind[p] is None else to_behind[p] + behind[p] for p in parts], "res", backward)
     mine = cols_sweep((0, 1), strip_tiles, integrals, held, fine, pieces=1)
-    second_other = cut(compact(second_other_rows))
-    second_scale = scales(late_index, (con_at * n_res + res_at) * fine)
     seconds = [
         (0.5 * second_other[p] + ((mine[p] + ahead[p]) + behind[p])) / second_scale[p] for p in parts
     ]
-    return expand(jnp.concatenate(firsts, axis=0)), expand(jnp.concatenate(seconds, axis=0))
+    return first_out, expand(jnp.concatenate(seconds, axis=0))
 
 
 def per_device(integrals, tile_mask, amplitudes, *rest):

time: 173 us -> 168 us (0.971)
  starting transfers between devices: 35 us -> 29.2 us
  waiting for transfers between devices: 44.4 us -> 47.5 us
    ppermute x34 -> x28, starting transfers between devices: 32.9 us -> 27.2 us  [send(): return [lax.ppermute(value, axis, perm) for value in values]]
    ppermute x34 -> x28, waiting for transfers between devices: 44.4 us -> 47.4 us  [send(): return [lax.ppermute(value, axis, perm) for value in values]]
    ppermute x1, starting transfers between devices: 2.01 us -> 0.06 us  [tiled(): lax.ppermute(far[p], 'res', onward)]
    ppermute x1, starting transfers between devices: 0.06 us -> 2.01 us  [tiled(): lax.ppermute(far[p], 'res', backward)]
    reduce_sum x2 -> x1, other arithmetic: 2.2 us -> 3.52 us  [vir_energies(): jnp.sum(jnp.where(picked[1][None, :] == orbitals, table, 0.0), axis=0)]
  transfers between devices with their start and end apart: 36 -> 30, of which waited for: 11 -> 9; matrix products, arithmetic and copies ran while one was open for 8% -> 8% of each run, Pallas kernels for 35% -> 36%
where the time goes in v1:
time: 168 us
  Pallas kernels  70 us (42%)
  waiting for transfers between devices  47.5 us (28%)
  starting transfers between devices  29.2 us (17%)
  matrix products  9.54 us (6%)
  other arithmetic  8.63 us (5%)
    pallas_call x9, Pallas kernels, sweep(): pl.pallas_call(functools.partial(sweep_kernel, by_rows, blocks, n_parts,...  70 us
    ppermute x28, waiting for transfers between devices, send(): return [lax.ppermute(value, axis, perm) for value in values]  47.4 us
    ppermute x28, starting transfers between devices, send(): return [lax.ppermute(value, axis, perm) for value in values]  27.2 us
    dot_general x2, matrix products, expand(): lax.dot_general(value, signed, (((0,), (0,)), ((), ())), precision=precis...  5.05 us
    dot_general x3, matrix products, compact(): lax.dot_general(signed, value, (((1,), (1,)), ((), ())), precision=precis...  4.29 us
    reduce_sum x1, other arithmetic, vir_energies(): jnp.sum(jnp.where(picked[1][None, :] == orbitals, table, 0.0), axis=0)  3.52 us
  transfers between devices with their start and end apart: 30, of which 9 were waited for; matrix products, arithmetic and copies ran while one was open for 8% of the time, Pallas kernels for 36%

profile of v1, /device:TPU:0, one launch (start us, length us, event | category | flops | bytes accessed | tf_op | source)
XLA Modules:
  0.0 167.5 jit_solution(7555259172763804911)
XLA Ops:
  3.8 3.1 %collective-permute-start = (f32[192,768]{1,0:T(8,128)S(1)}, f32[192,768]{1,0:T(8,128)S(1)}, u32[]{:S(2)}, u32[]{:S(2)}) collective-permute-start(f32[192,768]{1,0:T(8,128)S(1)} %fusion.8.refs_0_), channel_id=1, source_target_pairs={{0,2},{2,4},{4,6},{6,7},{7,5},{5,3},{3,1},{1,0},{8,10},{10,12},{12... | collective-permute-start | bytes 1769480 | tf_op jit(solution)/shard_map/ppermute | solution.py:307
  9.1 11.1 %collective-permute-done.refs_1_ = f32[192,768]{1,0:T(8,128)S(1)} collective-permute-done((f32[192,768]{1,0:T(8,128)S(1)}, f32[192,768]{1,0:T(8,128)S(1)}, u32[]{:S(2)}, u32[]{:S(2)}) %collective-permute-start) | collective-permute-done | bytes 589856 | tf_op jit(solution)/shard_map/ppermute | solution.py:307
  22.5 12.2 %collective-permute-done.1.refs_0_ = f32[192,768]{1,0:T(8,128)S(1)} collective-permute-done((f32[192,768]{1,0:T(8,128)S(1)}, f32[192,768]{1,0:T(8,128)S(1)}, u32[]{:S(2)}, u32[]{:S(2)}) %collective-permute-start.1) | collective-permute-done | bytes 589856 | tf_op jit(solution)/shard_map/ppermute | solution.py:307
  36.9 12.7 %rows_sweep.4.refs_2_ = f32[192,3072]{1,0:T(8,128)S(1)} custom-call(s32[9]{0:T(128)S(1)} %select_reduce_fusion.11.starts, s32[288]{0:T(512)S(1)} %get-tuple-element.79.row_of, s32[288]{0:T(512)S(1)} %select_reduce_fusion.10.col_of, s32[288]{0:T(512)S(1)} %get-tuple-element.86.strip_of, s32[288]{0:T(512)S(1)} %get-tuple-element.78.place_of, ...), custom_call_target="tpu_custom_call" | custom-call | flops 4076863488 | bytes 14155776 | tf_op jit(solution)/shard_map/rows_sweep/pallas_call | solution.py:184
  49.8 2.1 %collective-permute-start.7 = (f32[96,768]{1,0:T(8,128)S(1)}, f32[96,768]{1,0:T(8,128)S(1)}, u32[]{:S(2)}, u32[]{:S(2)}) collective-permute-start(f32[96,768]{1,0:T(8,128)S(1)} %slice.97), channel_id=1, source_target_pairs={{2,0},{4,2},{6,4},{7,6},{5,7},{3,5},{1,3},{0,1},{10,8},{12,10},{14... | collective-permute-start | bytes 884744 | tf_op jit(solution)/shard_map/ppermute | solution.py:307
  51.8 9.0 %rows_sweep.5.refs_2_ = f32[192,3072]{1,0:T(8,128)S(1)} custom-call(s32[9]{0:T(128)S(1)} %select_reduce_fusion.11.starts, s32[288]{0:T(512)S(1)} %get-tuple-element.79.row_of, s32[288]{0:T(512)S(1)} %select_reduce_fusion.10.col_of, s32[288]{0:T(512)S(1)} %get-tuple-element.86.strip_of, ...), custom_call_target="tpu_custom_call", output_to_operand_aliasing={{}: (8, {})} | custom-call | flops 2717908992 | bytes 9437184 | tf_op jit(solution)/shard_map/rows_sweep/pallas_call | solution.py:184
  60.9 8.1 %rows_sweep.6.refs_2_ = f32[192,3072]{1,0:T(8,128)S(1)} custom-call(s32[9]{0:T(128)S(1)} %select_reduce_fusion.11.starts, s32[288]{0:T(512)S(1)} %get-tuple-element.79.row_of, s32[288]{0:T(512)S(1)} %select_reduce_fusion.10.col_of, s32[288]{0:T(512)S(1)} %get-tuple-element.86.strip_of, ...), custom_call_target="tpu_custom_call", output_to_operand_aliasing={{}: (8, {})} | custom-call | flops 2717908992 | bytes 9437184 | tf_op jit(solution)/shard_map/rows_sweep/pallas_call | solution.py:184
  69.0 5.2 %rows_sweep.7 = (f32[96,1536]{1,0:T(8,128)S(1)}, f32[96,1536]{1,0:T(8,128)S(1)}, f32[96,1536]{1,0:T(8,128)S(1)}, f32[96,1536]{1,0:T(8,128)S(1)}) custom-call(s32[9]{0:T(128)S(1)} %select_reduce_fusion.11.starts, s32[288]{0:T(512)S(1)} %get-tuple-element.79.row_of, s32[288]{0:T(512)S(1)} %select_reduce_fusion.10.col_of, s32[288]{0:T(512)S(1)} %get-tuple-element.86.strip_of, ...), custom_call_target="tpu_custom_call" | custom-call | flops 1358954496 | bytes 4718592 | tf_op jit(solution)/shard_map/rows_sweep/pallas_call | solution.py:184
  78.2 2.1 %collective-permute-start.9 = (f32[96,768]{1,0:T(8,128)S(1)}, f32[96,768]{1,0:T(8,128)S(1)}, u32[]{:S(2)}, u32[]{:S(2)}) collective-permute-start(f32[96,768]{1,0:T(8,128)S(1)} %slice_add_fusion.3), channel_id=1, source_target_pairs={{0,16},{8,24},{16,0},{24,8},{1,17},{9,25},{17,1},{25,9},{2,18},{10... | collective-permute-start | bytes 884744 | tf_op jit(solution)/shard_map/ppermute | solution.py:307
  81.2 3.5 %select_reduce_fusion = (f32[768]{0:T(1024)S(1)}, f32[768]{0:T(1024)S(1)}, f32[768]{0:T(1024)S(1)}, f32[768]{0:T(1024)S(1)}) fusion(s32[768]{0:T(1024)S(1)} %get-tuple-element.64, f32[1600]{0:T(1024)S(1)} %copy-done.6, s32[768]{0:T(1024)S(1)} %get-tuple-element.67, s32[768]{0:T(1024)S(1)} %get-tuple-element.65, s32[768]{0:T(1024)S(1)} %get-tuple-element.66), kind=kLoop, calls=%fused_computation | loop fusion | flops 14742528 | bytes 30976 | tf_op jit(solution)/shard_map/reduce_sum | solution.py:255
  86.7 5.3 %collective-permute-done.9 = f32[96,768]{1,0:T(8,128)S(1)} collective-permute-done((f32[96,768]{1,0:T(8,128)S(1)}, f32[96,768]{1,0:T(8,128)S(1)}, u32[]{:S(2)}, u32[]{:S(2)}) %collective-permute-start.9) | collective-permute-done | bytes 294944 | tf_op jit(solution)/shard_map/ppermute | solution.py:307
  94.1 7.9 %collective-permute-done.13.refs_3_ = f32[96,768]{1,0:T(8,128)S(1)} collective-permute-done((f32[96,768]{1,0:T(8,128)S(1)}, f32[96,768]{1,0:T(8,128)S(1)}, u32[]{:S(2)}, u32[]{:S(2)}) %collective-permute-start.13) | collective-permute-done | bytes 294944 | tf_op jit(solution)/shard_map/ppermute | solution.py:307
  102.1 4.4 %collective-permute-done.12.refs_2_ = f32[96,768]{1,0:T(8,128)S(1)} collective-permute-done((f32[96,768]{1,0:T(8,128)S(1)}, f32[96,768]{1,0:T(8,128)S(1)}, u32[]{:S(2)}, u32[]{:S(2)}) %collective-permute-start.12) | collective-permute-done | bytes 294944 | tf_op jit(solution)/shard_map/ppermute | solution.py:307
  108.6 4.8 %cols_sweep.9 = (f32[96,768]{1,0:T(8,128)S(1)}, f32[96,768]{1,0:T(8,128)S(1)}) custom-call(s32[9]{0:T(128)S(1)} %select_reduce_fusion.11.starts, s32[288]{0:T(512)S(1)} %get-tuple-element.79.row_of, s32[288]{0:T(512)S(1)} %select_reduce_fusion.10.col_of, s32[288]{0:T(512)S(1)} %get-tuple-element.86.strip_of, s32[288]{0:T(512)S(1)} %get-tuple-element.78.place_of, ...), custom_call_target="tpu_custom_call" | custom-call | flops 1358954496 | bytes 4718592 | tf_op jit(solution)/shard_map/cols_sweep/pallas_call | solution.py:184
  115.5 7.6 %cols_sweep.8 = (f32[96,768]{1,0:T(8,128)S(1)}, f32[96,768]{1,0:T(8,128)S(1)}, f32[96,768]{1,0:T(8,128)S(1)}, f32[96,768]{1,0:T(8,128)S(1)}) custom-call(s32[9]{0:T(128)S(1)} %select_reduce_fusion.11.starts, s32[288]{0:T(512)S(1)} %get-tuple-element.79.row_of, s32[288]{0:T(512)S(1)} %select_reduce_fusion.10.col_of, s32[288]{0:T(512)S(1)} %get-tuple-element.86.strip_of, ...), custom_call_target="tpu_custom_call" | custom-call | flops 2717908992 | bytes 9437184 | tf_op jit(solution)/shard_map/cols_sweep/pallas_call | solution.py:184
  123.3 2.1 %collective-permute-start.17 = (f32[96,768]{1,0:T(8,128)S(1)}, f32[96,768]{1,0:T(8,128)S(1)}, u32[]{:S(2)}, u32[]{:S(2)}) collective-permute-start(f32[96,768]{1,0:T(8,128)S(1)} %add.174), channel_id=1, source_target_pairs={{0,2},{2,4},{4,6},{6,7},{7,5},{5,3},{3,1},{1,0},{8,10},{10,12},{12... | collective-permute-start | bytes 884744 | tf_op jit(solution)/shard_map/ppermute | solution.py:307
  127.5 8.5 %cols_sweep.7 = (f32[96,768]{1,0:T(8,128)S(1)}, f32[96,768]{1,0:T(8,128)S(1)}, f32[96,768]{1,0:T(8,128)S(1)}, f32[96,768]{1,0:T(8,128)S(1)}) custom-call(s32[9]{0:T(128)S(1)} %select_reduce_fusion.11.starts, s32[288]{0:T(512)S(1)} %get-tuple-element.79.row_of, s32[288]{0:T(512)S(1)} %select_reduce_fusion.10.col_of, s32[288]{0:T(512)S(1)} %get-tuple-element.86.strip_of, ...), custom_call_target="tpu_custom_call" | custom-call | flops 2717908992 | bytes 9437184 | tf_op jit(solution)/shard_map/cols_sweep/pallas_call | solution.py:184
  138.2 2.2 %collective-permute-done.23 = f32[96,768]{1,0:T(8,128)S(1)} collective-permute-done((f32[96,768]{1,0:T(8,128)S(1)}, f32[96,768]{1,0:T(8,128)S(1)}, u32[]{:S(2)}, u32[]{:S(2)}) %collective-permute-start.23) | collective-permute-done | bytes 294944 | tf_op jit(solution)/shard_map/ppermute | solution.py:307
  142.6 9.1 %cols_sweep.6 = (f32[96,768]{1,0:T(8,128)S(1)}, f32[96,768]{1,0:T(8,128)S(1)}, f32[96,768]{1,0:T(8,128)S(1)}, f32[96,768]{1,0:T(8,128)S(1)}) custom-call(s32[9]{0:T(128)S(1)} %select_reduce_fusion.11.starts, s32[288]{0:T(512)S(1)} %get-tuple-element.79.row_of, s32[288]{0:T(512)S(1)} %select_reduce_fusion.10.col_of, s32[288]{0:T(512)S(1)} %get-tuple-element.86.strip_of, ...), custom_call_target="tpu_custom_call" | custom-call | flops 2717908992 | bytes 9437184 | tf_op jit(solution)/shard_map/cols_sweep/pallas_call | solution.py:184
  151.9 2.3 %collective-permute-start.19 = (f32[96,768]{1,0:T(8,128)S(1)}, f32[96,768]{1,0:T(8,128)S(1)}, u32[]{:S(2)}, u32[]{:S(2)}) collective-permute-start(f32[96,768]{1,0:T(8,128)S(1)} %add.176), channel_id=1, source_target_pairs={{0,2},{2,4},{4,6},{6,7},{7,5},{5,3},{3,1},{1,0},{8,10},{10,12},{12... | collective-permute-start | bytes 884744 | tf_op jit(solution)/shard_map/ppermute | solution.py:307
  154.2 2.5 %fusion.2 = f32[768,384]{1,0:T(8,128)} fusion(f32[96,768]{1,0:T(8,128)S(1)} %fusion.19.refs_1_, f32[96,768]{1,0:T(8,128)S(1)} %fusion.23.refs_0_, f32[384]{0:T(512)S(1)} %get-tuple-element.76, s32[384]{0:T(512)S(1)} %select_reduce_fusion.4), kind=kOutput, calls=%fused_computation.11 | convolution fusion | flops 679772160 | bytes 1772544 | tf_op jit(solution)/shard_map/dot_general | solution.py:287
  156.9 2.1 %collective-permute-start.29 = (f32[96,768]{1,0:T(8,128)S(1)}, f32[96,768]{1,0:T(8,128)S(1)}, u32[]{:S(2)}, u32[]{:S(2)}) collective-permute-start(f32[96,768]{1,0:T(8,128)S(1)} %add.187), channel_id=1, source_target_pairs={{2,0},{4,2},{6,4},{7,6},{5,7},{3,5},{1,3},{0,1},{10,8},{12,10},{14... | collective-permute-start | bytes 884744 | tf_op jit(solution)/shard_map/ppermute | solution.py:307
  158.9 4.9 %cols_sweep.5 = (f32[96,768]{1,0:T(8,128)S(1)}, f32[96,768]{1,0:T(8,128)S(1)}) custom-call(s32[9]{0:T(128)S(1)} %select_reduce_fusion.11.starts, s32[288]{0:T(512)S(1)} %get-tuple-element.79.row_of, s32[288]{0:T(512)S(1)} %select_reduce_fusion.10.col_of, s32[288]{0:T(512)S(1)} %get-tuple-element.86.strip_of, s32[288]{0:T(512)S(1)} %get-tuple-element.78.place_of, ...), custom_call_target="tpu_custom_call" | custom-call | flops 1358954496 | bytes 4718592 | tf_op jit(solution)/shard_map/cols_sweep/pallas_call | solution.py:184
  165.0 2.5 %fusion = f32[768,384]{1,0:T(8,128)} fusion(f32[96,768]{1,0:T(8,128)S(1)} %add_divide_fusion, f32[96,768]{1,0:T(8,128)S(1)} %add_divide_fusion.1, f32[384]{0:T(512)S(1)} %get-tuple-element.76, s32[384]{0:T(512)S(1)} %select_reduce_fusion.4), kind=kOutput, calls=%fused_computation.9 | convolution fusion | flops 679772160 | bytes 1772544 | tf_op jit(solution)/shard_map/dot_general | solution.py:287
  (119 shorter events, 31.2 us)
Async XLA Ops:
  3.8 16.4 %collective-permute-start = (f32[192,768]{1,0:T(8,128)S(1)}, f32[192,768]{1,0:T(8,128)S(1)}, u32[]{:S(2)}, u32[]{:S(2)}) collective-permute-start(f32[192,768]{1,0:T(8,128)S(1)} %fusion.8.refs_0_), channel_id=1, source_target_pairs={{0,2},{2,4},{4,6},{6,7},{7,5},{5,3},{3,1},{1,0},{8,10},{10,12},{12... | collective-permute-start | bytes 1769480 | tf_op jit(solution)/shard_map/ppermute | solution.py:307
  6.9 15.1 %collective-permute-start.4 = (f32[192,768]{1,0:T(8,128)S(1)}, f32[192,768]{1,0:T(8,128)S(1)}, u32[]{:S(2)}, u32[]{:S(2)}) collective-permute-start(f32[192,768]{1,0:T(8,128)S(1)} %fusion.8.refs_0_), channel_id=1, source_target_pairs={{2,0},{4,2},{6,4},{7,6},{5,7},{3,5},{1,3},{0,1},{10,8},{12,10},{14... | collective-permute-start | bytes 1769480 | tf_op jit(solution)/shard_map/ppermute | solution.py:307
  20.2 14.5 %collective-permute-start.1 = (f32[192,768]{1,0:T(8,128)S(1)}, f32[192,768]{1,0:T(8,128)S(1)}, u32[]{:S(2)}, u32[]{:S(2)}) collective-permute-start(f32[192,768]{1,0:T(8,128)S(1)} %collective-permute-done.refs_1_), channel_id=1, source_target_pairs={{0,2},{2,4},{4,6},{6,7},{7,5},{5,3},{3,1},{1,0},{8,10},{10,12},{12... | collective-permute-start | bytes 1769480 | tf_op jit(solution)/shard_map/ppermute | solution.py:307
  22.0 14.2 %collective-permute-start.5 = (f32[192,768]{1,0:T(8,128)S(1)}, f32[192,768]{1,0:T(8,128)S(1)}, u32[]{:S(2)}, u32[]{:S(2)}) collective-permute-start(f32[192,768]{1,0:T(8,128)S(1)} %collective-permute-done.4.refs_2_), channel_id=1, source_target_pairs={{2,0},{4,2},{6,4},{7,6},{5,7},{3,5},{1,3},{0,1},{10,8},{12,10},{14... | collective-permute-start | bytes 1769480 | tf_op jit(solution)/shard_map/ppermute | solution.py:307
  34.7 15.0 %collective-permute-start.2 = (f32[192,768]{1,0:T(8,128)S(1)}, f32[192,768]{1,0:T(8,128)S(1)}, u32[]{:S(2)}, u32[]{:S(2)}) collective-permute-start(f32[192,768]{1,0:T(8,128)S(1)} %collective-permute-done.1.refs_0_), channel_id=1, source_target_pairs={{0,2},{2,4},{4,6},{6,7},{7,5},{5,3},{3,1},{1,0},{8,10},{10,12},{12... | collective-permute-start | bytes 1769480 | tf_op jit(solution)/shard_map/ppermute | solution.py:307
  36.2 13.6 %collective-permute-start.6 = (f32[192,768]{1,0:T(8,128)S(1)}, f32[192,768]{1,0:T(8,128)S(1)}, u32[]{:S(2)}, u32[]{:S(2)}) collective-permute-start(f32[192,768]{1,0:T(8,128)S(1)} %collective-permute-done.5.refs_1_), channel_id=1, source_target_pairs={{2,0},{4,2},{6,4},{7,6},{5,7},{3,5},{1,3},{0,1},{10,8},{12,10},{14... | collective-permute-start | bytes 1769480 | tf_op jit(solution)/shard_map/ppermute | solution.py:307
  49.7 19.3 %collective-permute-start.3 = (f32[96,768]{1,0:T(8,128)S(1)}, f32[96,768]{1,0:T(8,128)S(1)}, u32[]{:S(2)}, u32[]{:S(2)}) collective-permute-start(f32[96,768]{1,0:T(8,128)S(1)} %slice.96), channel_id=1, source_target_pairs={{0,2},{2,4},{4,6},{6,7},{7,5},{5,3},{3,1},{1,0},{8,10},{10,12},{12... | collective-permute-start | bytes 884744 | tf_op jit(solution)/shard_map/ppermute | solution.py:307
  49.8 19.2 %collective-permute-start.7 = (f32[96,768]{1,0:T(8,128)S(1)}, f32[96,768]{1,0:T(8,128)S(1)}, u32[]{:S(2)}, u32[]{:S(2)}) collective-permute-start(f32[96,768]{1,0:T(8,128)S(1)} %slice.97), channel_id=1, source_target_pairs={{2,0},{4,2},{6,4},{7,6},{5,7},{3,5},{1,3},{0,1},{10,8},{12,10},{14... | collective-permute-start | bytes 884744 | tf_op jit(solution)/shard_map/ppermute | solution.py:307
  76.6 9.9 %collective-permute-start.11 = (f32[96,768]{1,0:T(8,128)S(1)}, f32[96,768]{1,0:T(8,128)S(1)}, u32[]{:S(2)}, u32[]{:S(2)}) collective-permute-start(f32[96,768]{1,0:T(8,128)S(1)} %slice_add_fusion.1), channel_id=1, source_target_pairs={{0,16},{8,24},{16,0},{24,8},{1,17},{9,25},{17,1},{25,9},{2,18},{10... | collective-permute-start | bytes 884744 | tf_op jit(solution)/shard_map/ppermute | solution.py:307
  78.2 13.7 %collective-permute-start.9 = (f32[96,768]{1,0:T(8,128)S(1)}, f32[96,768]{1,0:T(8,128)S(1)}, u32[]{:S(2)}, u32[]{:S(2)}) collective-permute-start(f32[96,768]{1,0:T(8,128)S(1)} %slice_add_fusion.3), channel_id=1, source_target_pairs={{0,16},{8,24},{16,0},{24,8},{1,17},{9,25},{17,1},{25,9},{2,18},{10... | collective-permute-start | bytes 884744 | tf_op jit(solution)/shard_map/ppermute | solution.py:307
  92.0 9.9 %collective-permute-start.13 = (f32[96,768]{1,0:T(8,128)S(1)}, f32[96,768]{1,0:T(8,128)S(1)}, u32[]{:S(2)}, u32[]{:S(2)}) collective-permute-start(f32[96,768]{1,0:T(8,128)S(1)} %fusion.19.refs_1_), channel_id=1, source_target_pairs={{0,16},{8,24},{16,0},{24,8},{1,17},{9,25},{17,1},{25,9},{2,18},{10... | collective-permute-start | bytes 884744 | tf_op jit(solution)/shard_map/ppermute | solution.py:307
  92.4 14.1 %collective-permute-start.12 = (f32[96,768]{1,0:T(8,128)S(1)}, f32[96,768]{1,0:T(8,128)S(1)}, u32[]{:S(2)}, u32[]{:S(2)}) collective-permute-start(f32[96,768]{1,0:T(8,128)S(1)} %fusion.23.refs_0_), channel_id=1, source_target_pairs={{0,16},{8,24},{16,0},{24,8},{1,17},{9,25},{17,1},{25,9},{2,18},{10... | collective-permute-start | bytes 884744 | tf_op jit(solution)/shard_map/ppermute | solution.py:307
  113.5 9.8 %collective-permute-start.16 = (f32[96,768]{1,0:T(8,128)S(1)}, f32[96,768]{1,0:T(8,128)S(1)}, u32[]{:S(2)}, u32[]{:S(2)}) collective-permute-start(f32[96,768]{1,0:T(8,128)S(1)} %get-tuple-element.49), channel_id=1, source_target_pairs={{0,2},{2,4},{4,6},{6,7},{7,5},{5,3},{3,1},{1,0},{8,10},{10,12},{12... | collective-permute-start | bytes 884744 | tf_op jit(solution)/shard_map/ppermute | solution.py:357
  113.5 11.9 %collective-permute-start.26 = (f32[96,768]{1,0:T(8,128)S(1)}, f32[96,768]{1,0:T(8,128)S(1)}, u32[]{:S(2)}, u32[]{:S(2)}) collective-permute-start(f32[96,768]{1,0:T(8,128)S(1)} %get-tuple-element.62), channel_id=1, source_target_pairs={{2,0},{4,2},{6,4},{7,6},{5,7},{3,5},{1,3},{0,1},{10,8},{12,10},{14... | collective-permute-start | bytes 884744 | tf_op jit(solution)/shard_map/ppermute | solution.py:358
  123.2 12.8 %collective-permute-start.20 = (f32[96,768]{1,0:T(8,128)S(1)}, f32[96,768]{1,0:T(8,128)S(1)}, u32[]{:S(2)}, u32[]{:S(2)}) collective-permute-start(f32[96,768]{1,0:T(8,128)S(1)} %get-tuple-element.52), channel_id=1, source_target_pairs={{2,0},{4,2},{6,4},{7,6},{5,7},{3,5},{1,3},{0,1},{10,8},{12,10},{14... | collective-permute-start | bytes 884744 | tf_op jit(solution)/shard_map/ppermute | solution.py:307
  123.3 12.8 %collective-permute-start.17 = (f32[96,768]{1,0:T(8,128)S(1)}, f32[96,768]{1,0:T(8,128)S(1)}, u32[]{:S(2)}, u32[]{:S(2)}) collective-permute-start(f32[96,768]{1,0:T(8,128)S(1)} %add.174), channel_id=1, source_target_pairs={{0,2},{2,4},{4,6},{6,7},{7,5},{5,3},{3,1},{1,0},{8,10},{10,12},{12... | collective-permute-start | bytes 884744 | tf_op jit(solution)/shard_map/ppermute | solution.py:307
  125.4 15.0 %collective-permute-start.23 = (f32[96,768]{1,0:T(8,128)S(1)}, f32[96,768]{1,0:T(8,128)S(1)}, u32[]{:S(2)}, u32[]{:S(2)}) collective-permute-start(f32[96,768]{1,0:T(8,128)S(1)} %get-tuple-element.58), channel_id=1, source_target_pairs={{0,2},{2,4},{4,6},{6,7},{7,5},{5,3},{3,1},{1,0},{8,10},{10,12},{12... | collective-permute-start | bytes 884744 | tf_op jit(solution)/shard_map/ppermute | solution.py:307
  125.5 16.2 %collective-permute-start.27 = (f32[96,768]{1,0:T(8,128)S(1)}, f32[96,768]{1,0:T(8,128)S(1)}, u32[]{:S(2)}, u32[]{:S(2)}) collective-permute-start(f32[96,768]{1,0:T(8,128)S(1)} %add.185), channel_id=1, source_target_pairs={{2,0},{4,2},{6,4},{7,6},{5,7},{3,5},{1,3},{0,1},{10,8},{12,10},{14... | collective-permute-start | bytes 884744 | tf_op jit(solution)/shard_map/ppermute | solution.py:307
  136.1 15.7 %collective-permute-start.21 = (f32[96,768]{1,0:T(8,128)S(1)}, f32[96,768]{1,0:T(8,128)S(1)}, u32[]{:S(2)}, u32[]{:S(2)}) collective-permute-start(f32[96,768]{1,0:T(8,128)S(1)} %add.178), channel_id=1, source_target_pairs={{2,0},{4,2},{6,4},{7,6},{5,7},{3,5},{1,3},{0,1},{10,8},{12,10},{14... | collective-permute-start | bytes 884744 | tf_op jit(solution)/shard_map/ppermute | solution.py:307
  136.2 15.7 %collective-permute-start.18 = (f32[96,768]{1,0:T(8,128)S(1)}, f32[96,768]{1,0:T(8,128)S(1)}, u32[]{:S(2)}, u32[]{:S(2)}) collective-permute-start(f32[96,768]{1,0:T(8,128)S(1)} %add.175), channel_id=1, source_target_pairs={{0,2},{2,4},{4,6},{6,7},{7,5},{5,3},{3,1},{1,0},{8,10},{10,12},{12... | collective-permute-start | bytes 884744 | tf_op jit(solution)/shard_map/ppermute | solution.py:307
  140.4 16.3 %collective-permute-start.24 = (f32[96,768]{1,0:T(8,128)S(1)}, f32[96,768]{1,0:T(8,128)S(1)}, u32[]{:S(2)}, u32[]{:S(2)}) collective-permute-start(f32[96,768]{1,0:T(8,128)S(1)} %add.182), channel_id=1, source_target_pairs={{0,2},{2,4},{4,6},{6,7},{7,5},{5,3},{3,1},{1,0},{8,10},{10,12},{12... | collective-permute-start | bytes 884744 | tf_op jit(solution)/shard_map/ppermute | solution.py:307
  141.7 15.1 %collective-permute-start.28 = (f32[96,768]{1,0:T(8,128)S(1)}, f32[96,768]{1,0:T(8,128)S(1)}, u32[]{:S(2)}, u32[]{:S(2)}) collective-permute-start(f32[96,768]{1,0:T(8,128)S(1)} %add.186), channel_id=1, source_target_pairs={{2,0},{4,2},{6,4},{7,6},{5,7},{3,5},{1,3},{0,1},{10,8},{12,10},{14... | collective-permute-start | bytes 884744 | tf_op jit(solution)/shard_map/ppermute | solution.py:307
  151.8 12.0 %collective-permute-start.22 = (f32[96,768]{1,0:T(8,128)S(1)}, f32[96,768]{1,0:T(8,128)S(1)}, u32[]{:S(2)}, u32[]{:S(2)}) collective-permute-start(f32[96,768]{1,0:T(8,128)S(1)} %add.179), channel_id=1, source_target_pairs={{2,0},{4,2},{6,4},{7,6},{5,7},{3,5},{1,3},{0,1},{10,8},{12,10},{14... | collective-permute-start | bytes 884744 | tf_op jit(solution)/shard_map/ppermute | solution.py:307
  151.9 11.9 %collective-permute-start.19 = (f32[96,768]{1,0:T(8,128)S(1)}, f32[96,768]{1,0:T(8,128)S(1)}, u32[]{:S(2)}, u32[]{:S(2)}) collective-permute-start(f32[96,768]{1,0:T(8,128)S(1)} %add.176), channel_id=1, source_target_pairs={{0,2},{2,4},{4,6},{6,7},{7,5},{5,3},{3,1},{1,0},{8,10},{10,12},{12... | collective-permute-start | bytes 884744 | tf_op jit(solution)/shard_map/ppermute | solution.py:307
  (15 other events, 73.4 us)

commit v2 on v1

--- a/solution.py
+++ b/solution.py
@@ -80,16 +80,25 @@
     return high, (value - high.astype(f32)).astype(bf16)
 
 
-def sweep_kernel(by_rows, blocks, n_parts, has_start, n_out, strip_base, edge, starts, row_of, col_of, strip_of, place_of, a_hbm, *refs):
+def sweep_kernel(
+    by_rows, blocks, n_parts, has_start, n_out, keeps, strip_base, edge,
+    starts, row_of, col_of, strip_of, place_of, a_hbm, *refs,
+):
     n_x = len(blocks) * n_parts
     x_refs = refs[:n_x]
     start_ref = refs[n_x] if has_start else None
     refs = refs[n_x + has_start :]
+    if not blocks:
+        x_split, refs = refs[0], refs[1:]
     out_refs, refs = refs[:n_out], refs[n_out:]
+    if keeps:
+        x_split, refs = refs[0], refs[1:]
     y_ref = out_refs[0] if n_out == 1 else refs[0]
     refs = refs if n_out == 1 else refs[1:]
-    x_split, tiles, sems, x_sem = refs[:4]
-    x_whole = refs[4:]
+    tiles, sems, x_sem = refs[:3]
+    x_whole = refs[3:]
+    if blocks and not keeps:
+        x_split, x_whole = x_whole[0], x_whole[1:]
     first = starts[edge[0]]
     count = starts[edge[1]] - first
 
@@ -167,34 +176,40 @@
             out_ref[...] = y_ref[p * part_rows : (p + 1) * part_rows, c * out_cols : (c + 1) * out_cols]
 
 
-def sweep(by_rows, tables, starts, edge, strip_tiles, integrals, x_blocks, y_width, start=None, pieces=0):
-    n_parts = len(x_blocks[0])
-    part_rows = x_blocks[0][0].shape[0]
-    width = n_parts * part_rows
-    blocks = [block[0].shape[1] for block in x_blocks]
-    inputs = [part for block in x_blocks for part in block]
+def sweep(
+    by_rows, tables, starts, edge, strip_tiles, integrals, x_blocks, y_width, start=None, pieces=0, split=None, keeps=False
+):
+    n_parts = len(x_blocks[0]) if split is None else PARTS
+    width = sum(part.shape[0] for part in x_blocks[0]) if split is None else split.shape[1] // 2
+    blocks = [block[0].shape[1] for block in x_blocks] if split is None else []
+    inputs = [part for block in x_blocks for part in block] if split is None else []
     scalar = pl.BlockSpec(memory_space=pltpu.SMEM)
     vector = pl.BlockSpec(memory_space=pltpu.VMEM)
     anywhere = pl.BlockSpec(memory_space=pl.ANY)
     has_start = start is not None
     n_out = pieces * n_parts if pieces else 1
-    whole = jax.ShapeDtypeStruct((width, y_width), f32)
     tile_guess = (edge[1] - edge[0]) * strip_tiles * (integrals.shape[0] // W) // 2
-    extra = [pltpu.VMEM((width, y_width), f32)] if pieces else []
-    return pl.pallas_call(
+    split_shape = (sum(blocks) // W, 2 * width, W)
+    out_shape = [jax.ShapeDtypeStruct((width, y_width), f32)]
+    if pieces:
+        out_shape = [jax.ShapeDtypeStruct((width // n_parts, y_width // pieces), f32)] * n_out
+    if keeps:
+        out_shape += [jax.ShapeDtypeStruct(split_shape, bf16)]
+    late = ([start] if has_start else []) + ([] if split is None else [split])
+    out = pl.pallas_call(
         functools.partial(
-            sweep_kernel, by_rows, blocks, n_parts, int(has_start), n_out, edge[0] * strip_tiles, edge
+            sweep_kernel, by_rows, blocks, n_parts, int(has_start), n_out, keeps, edge[0] * strip_tiles, edge
         ),
-        out_shape=[jax.ShapeDtypeStruct((part_rows, y_width // pieces), f32)] * n_out if pieces else whole,
-        in_specs=[scalar] * 5 + [anywhere] * (1 + len(inputs)) + [vector] * has_start,
-        out_specs=[vector] * n_out if pieces else vector,
-        scratch_shapes=extra
+        out_shape=out_shape,
+        in_specs=[scalar] * 5 + [anywhere] * (1 + len(inputs)) + [vector] * len(late),
+        out_specs=[vector] * len(out_shape),
+        scratch_shapes=([pltpu.VMEM((width, y_width), f32)] if n_out > 1 else [])
         + [
-            pltpu.VMEM((sum(blocks) // W, 2 * width, W), bf16),
             pltpu.VMEM((DEPTH, W, W), f32),
             pltpu.SemaphoreType.DMA((DEPTH,)),
-            pltpu.SemaphoreType.DMA((len(inputs),)),
+            pltpu.SemaphoreType.DMA((max(len(inputs), 1),)),
         ]
+        + ([pltpu.VMEM(split_shape, bf16)] if blocks and not keeps else [])
         + [pltpu.VMEM((width, n), f32) for n in blocks],
         input_output_aliases={6 + len(inputs): 0} if has_start and not pieces else {},
         compiler_params=pltpu.CompilerParams(vmem_limit_bytes=32 * 2**20),
@@ -202,7 +217,8 @@
             flops=6 * width * W * W * tile_guess, bytes_accessed=4 * W * W * tile_guess, transcendentals=0
         ),
         name="rows_sweep" if by_rows else "cols_sweep",
-    )(starts, *tables, integrals, *inputs, *([start] if has_start else []))
+    )(starts, *tables, integrals, *inputs, *late)
+    return out if len(out) > 1 else out[0]
 
 
 def ring_order(n):
@@ -310,21 +326,18 @@
         return cut(vir_energies(index, eps_vir, offset, fine)[None, :] - occ_pair[:, None])
 
     near = n_res // 2
-    own = [compact(amplitudes)]
+    own = cut(compact(amplitudes))
+    first_other, second_other = compact(other_first), compact(other_second)
     ahead = behind = own
-    blocks = [own]
-    ladder = None
+    ladder = rows_sweep((0, 1), strip_tiles, integrals, [own], rows)
     for s in range(1, near):
         ahead, behind = send(ahead, "res", onward), send(behind, "res", backward)
-        blocks += [ahead, behind]
-        edge = (2 * s + 1 - len(blocks), 2 * s + 1)
-        ladder = rows_sweep(edge, strip_tiles, integrals, blocks, rows, ladder)
-        blocks = []
-    far = send(cut(ahead[0])[: PARTS // 2], "res", onward)
-    far += send(cut(behind[0])[PARTS // 2 :], "res", backward)
+        ahead, behind = lax.optimization_barrier((ahead, behind))
+        ladder = rows_sweep((2 * s - 1, 2 * s + 1), strip_tiles, integrals, [ahead, behind], rows, ladder)
+    far = send(ahead[: PARTS // 2], "res", onward)
+    far += send(behind[PARTS // 2 :], "res", backward)
     pieces = rows_sweep((n_res - 1, n_res), strip_tiles, integrals, [far], rows, ladder, pieces=2)
     kept, sent = pieces[:PARTS], pieces[PARTS:]
-    first_other = compact(other_first)
     bit = 1
     while bit < n_con:
         swap = [(i, i ^ bit) for i in range(n_con)]
@@ -334,13 +347,12 @@
             mid = kept[0].shape[1] // 2
             sent = [kept[p][:, mid:] + came[p][:, mid:] for p in parts]
             kept = [kept[p][:, :mid] + came[p][:, :mid] for p in parts]
-            late_index, late_other, sent[0] = lax.optimization_barrier((vir_index, other_second, sent[0]))
+            late_index, sent[0] = lax.optimization_barrier((vir_index, sent[0]))
     ready = (
         scales(late_index, (res_at * n_con + con_at) * fine),
         scales(late_index, (con_at * n_res + res_at) * fine),
-        cut(compact(late_other)),
-    )
-    first_scale, second_scale, second_other = lax.optimization_barrier(ready)
+    )
+    first_scale, second_scale = lax.optimization_barrier(ready)
     firsts = []
     for p, part in enumerate(cut(first_other)):
         if firsts:
@@ -353,16 +365,17 @@
         block = [jnp.concatenate([h[p] for h in held], axis=1) if len(held) > 1 else held[0][p] for p in parts]
         held = held + [send(block[:-1], "con", swap) + send(block[-1:], "con", swap)]
     first_out = expand(jnp.concatenate(firsts, axis=0))
-    far = cols_sweep((n_res - 1, n_res), strip_tiles, integrals, held, fine, pieces=1)
+    *far, split = cols_sweep((n_res - 1, n_res), strip_tiles, integrals, held, fine, pieces=1, keeps=True)
     ahead = [lax.ppermute(far[p], "res", onward) if p < PARTS // 2 else None for p in parts]
     behind = [None if p < PARTS // 2 else lax.ppermute(far[p], "res", backward) for p in parts]
     for s in range(near - 1, 0, -1):
         edge = (2 * s - 1, 2 * s + 1)
-        both = cols_sweep(edge, strip_tiles, integrals, held, 2 * fine, pieces=2)
+        both = cols_sweep(edge, strip_tiles, integrals, None, 2 * fine, pieces=2, split=split)
         to_behind, to_ahead = both[:PARTS], both[PARTS:]
         ahead = send([to_ahead[p] if ahead[p] is None else to_ahead[p] + ahead[p] for p in parts], "res", onward)
         behind = send([to_behind[p] if behind[p] is None else to_behind[p] + behind[p] for p in parts], "res", backward)
-    mine = cols_sweep((0, 1), strip_tiles, integrals, held, fine, pieces=1)
+    mine = cols_sweep((0, 1), strip_tiles, integrals, None, fine, pieces=1, split=split)
+    second_other = cut(second_other)
     seconds = [
         (0.5 * second_other[p] + ((mine[p] + ahead[p]) + behind[p])) / second_scale[p] for p in parts
     ]

time: 168 us -> 185 us (1.10)
  local copies, waits for them, and re-layouts: 1.46 us -> 12.1 us
  starting transfers between devices: 29.2 us -> 34.9 us
    unnamed x18 -> x58, local copies, waits for them, and re-layouts: 0.06 us -> 10.8 us
    ppermute x28 -> x34, starting transfers between devices: 27.2 us -> 32.8 us  [send(): return [lax.ppermute(value, axis, perm) for value in values]]
    ppermute x1, starting transfers between devices: 2.01 us -> 0.06 us  [tiled(): lax.ppermute(far[p], 'res', backward)]
    ppermute x1, starting transfers between devices: 0.06 us -> 2.01 us  [tiled(): lax.ppermute(far[p], 'res', onward)]
    pallas_call x9 -> x10, Pallas kernels: 70 us -> 71.7 us  [sweep(): pl.pallas_call(functools.partial(sweep_kernel, by_rows, blocks, n_parts,...]
    ppermute x28 -> x34, waiting for transfers between devices: 47.4 us -> 46.1 us  [send(): return [lax.ppermute(value, axis, perm) for value in values]]
  transfers between devices with their start and end apart: 30 -> 36, of which waited for: 9 -> 15; matrix products, arithmetic and copies ran while one was open for 8% -> 7% of each run, Pallas kernels for 36% -> 33%
where the time goes in v2:
time: 185 us; the launch traced here: 184 us
  Pallas kernels  71.7 us (39%)
  waiting for transfers between devices  46.1 us (25%)
  starting transfers between devices  34.9 us (19%)
  local copies, waits for them, and re-layouts  12.1 us (7%)
  matrix products  9.53 us (5%)
  other arithmetic  8.7 us (5%)
    pallas_call x10, Pallas kernels, sweep(): pl.pallas_call(functools.partial(sweep_kernel, by_rows, blocks, n_parts,...  71.7 us
    ppermute x34, waiting for transfers between devices, send(): return [lax.ppermute(value, axis, perm) for value in values]  46.1 us
    ppermute x34, starting transfers between devices, send(): return [lax.ppermute(value, axis, perm) for value in values]  32.8 us
    unnamed x58, local copies, waits for them, and re-layouts  10.8 us
    dot_general x2, matrix products, expand(): lax.dot_general(value, signed, (((0,), (0,)), ((), ())), precision=precis...  5.06 us
    dot_general x3, matrix products, compact(): lax.dot_general(signed, value, (((1,), (1,)), ((), ())), precision=precis...  4.28 us
  transfers between devices with their start and end apart: 36, of which 15 were waited for; matrix products, arithmetic and copies ran while one was open for 7% of the time, Pallas kernels for 33%

profile of v2, /device:TPU:0, one launch (start us, length us, event | category | flops | bytes accessed | tf_op | source)
XLA Modules:
  0.0 184.4 jit_solution(602497709900486238)
XLA Ops:
  3.9 3.1 %collective-permute-start = (f32[96,768]{1,0:T(8,128)S(1)}, f32[96,768]{1,0:T(8,128)S(1)}, u32[]{:S(2)}, u32[]{:S(2)}) collective-permute-start(f32[96,768]{1,0:T(8,128)S(1)} %get-tuple-element.107.refs_0_), channel_id=1, source_target_pairs={{0,2},{2,4},{4,6},{6,7},{7,5},{5,3},{3,1},{1,0},{8,10},{10,12},{12... | collective-permute-start | bytes 884744 | tf_op jit(solution)/shard_map/ppermute | solution.py:323
  14.8 5.5 %collective-permute-done.1.refs_1_ = f32[96,768]{1,0:T(8,128)S(1)} collective-permute-done((f32[96,768]{1,0:T(8,128)S(1)}, f32[96,768]{1,0:T(8,128)S(1)}, u32[]{:S(2)}, u32[]{:S(2)}) %collective-permute-start.1) | collective-permute-done | bytes 294944 | tf_op jit(solution)/shard_map/ppermute | solution.py:323
  29.0 2.8 %collective-permute-done.4.refs_0_ = f32[96,768]{1,0:T(8,128)} collective-permute-done((f32[96,768]{1,0:T(8,128)S(1)}, f32[96,768]{1,0:T(8,128)}, u32[]{:S(2)}, u32[]{:S(2)}) %collective-permute-start.4) | collective-permute-done | bytes 294944 | tf_op jit(solution)/shard_map/ppermute | solution.py:323
  31.8 4.1 %collective-permute-done.5.refs_1_ = f32[96,768]{1,0:T(8,128)} collective-permute-done((f32[96,768]{1,0:T(8,128)S(1)}, f32[96,768]{1,0:T(8,128)}, u32[]{:S(2)}, u32[]{:S(2)}) %collective-permute-start.5) | collective-permute-done | bytes 294944 | tf_op jit(solution)/shard_map/ppermute | solution.py:323
  36.3 3.5 %collective-permute-done.7.refs_3_ = f32[96,768]{1,0:T(8,128)} collective-permute-done((f32[96,768]{1,0:T(8,128)S(1)}, f32[96,768]{1,0:T(8,128)}, u32[]{:S(2)}, u32[]{:S(2)}) %collective-permute-start.7) | collective-permute-done | bytes 294944 | tf_op jit(solution)/shard_map/ppermute | solution.py:323
  45.8 5.0 %rows_sweep.5.refs_4_ = f32[192,3072]{1,0:T(8,128)S(1)} custom-call(s32[9]{0:T(128)S(1)} %select_reduce_fusion.11.starts, s32[288]{0:T(512)S(1)} %get-tuple-element.99.row_of, s32[288]{0:T(512)S(1)} %select_reduce_fusion.10.col_of, s32[288]{0:T(512)S(1)} %get-tuple-element.108.strip_of, s32[288]{0:T(512)S(1)} %get-tuple-element.98.place_of, ...), custom_call_target="tpu_custom_call" | custom-call | flops 1358954496 | bytes 4718592 | tf_op jit(solution)/shard_map/rows_sweep/pallas_call | solution.py:199
  55.3 9.7 %rows_sweep.6.refs_4_ = f32[192,3072]{1,0:T(8,128)S(1)} custom-call(s32[9]{0:T(128)S(1)} %copy-done.14, s32[288]{0:T(512)S(1)} %get-tuple-element.99.row_of, s32[288]{0:T(512)S(1)} %select_reduce_fusion.10.col_of, s32[288]{0:T(512)S(1)} %get-tuple-element.108.strip_of, s32[288]{0:T(512)S(1)} %get-tuple-element.98.place_of, ...), custom_call_target="tpu_custom_call", output_to_operand_aliasing={{}: (10, {})} | custom-call | flops 2717908992 | bytes 9437184 | tf_op jit(solution)/shard_map/rows_sweep/pallas_call | solution.py:199
  67.1 9.7 %rows_sweep.7.refs_4_ = f32[192,3072]{1,0:T(8,128)S(1)} custom-call(s32[9]{0:T(128)S(1)} %copy-done.14, s32[288]{0:T(512)S(1)} %get-tuple-element.99.row_of, s32[288]{0:T(512)S(1)} %select_reduce_fusion.10.col_of, s32[288]{0:T(512)S(1)} %get-tuple-element.108.strip_of, s32[288]{0:T(512)S(1)} %get-tuple-element.98.place_of, ...), custom_call_target="tpu_custom_call", output_to_operand_aliasing={{}: (10, {})} | custom-call | flops 2717908992 | bytes 9437184 | tf_op jit(solution)/shard_map/rows_sweep/pallas_call | solution.py:199
  76.8 8.7 %rows_sweep.8.refs_2_ = f32[192,3072]{1,0:T(8,128)S(1)} custom-call(s32[9]{0:T(128)S(1)} %copy-done.14, s32[288]{0:T(512)S(1)} %get-tuple-element.99.row_of, s32[288]{0:T(512)S(1)} %select_reduce_fusion.10.col_of, s32[288]{0:T(512)S(1)} %get-tuple-element.108.strip_of, s32[288]{0:T(512)S(1)} %get-tuple-element.98.place_of, ...), custom_call_target="tpu_custom_call", output_to_operand_aliasing={{}: (10, {})} | custom-call | flops 2717908992 | bytes 9437184 | tf_op jit(solution)/shard_map/rows_sweep/pallas_call | solution.py:199
  85.6 5.2 %rows_sweep.9 = (f32[96,1536]{1,0:T(8,128)S(1)}, f32[96,1536]{1,0:T(8,128)S(1)}, f32[96,1536]{1,0:T(8,128)S(1)}, f32[96,1536]{1,0:T(8,128)S(1)}) custom-call(s32[9]{0:T(128)S(1)} %copy-done.14, s32[288]{0:T(512)S(1)} %get-tuple-element.99.row_of, s32[288]{0:T(512)S(1)} %select_reduce_fusion.10.col_of, s32[288]{0:T(512)S(1)} %get-tuple-element.108.strip_of, ...), custom_call_target="tpu_custom_call" | custom-call | flops 1358954496 | bytes 4718592 | tf_op jit(solution)/shard_map/rows_sweep/pallas_call | solution.py:199
  96.4 3.5 %select_reduce_fusion = (f32[768]{0:T(1024)S(1)}, f32[768]{0:T(1024)S(1)}, f32[768]{0:T(1024)S(1)}, f32[768]{0:T(1024)S(1)}) fusion(s32[768]{0:T(1024)S(1)} %get-tuple-element.84, f32[1600]{0:T(1024)S(1)} %copy-done.26, s32[768]{0:T(1024)S(1)} %get-tuple-element.87, s32[768]{0:T(1024)S(1)} %get-tuple-element.85, s32[768]{0:T(1024)S(1)} %get-tuple-element.86), kind=kLoop, calls=%fused_computation | loop fusion | flops 14742528 | bytes 30976 | tf_op jit(solution)/shard_map/reduce_sum | solution.py:271
  100.2 3.0 %collective-permute-done.17 = f32[96,768]{1,0:T(8,128)S(1)} collective-permute-done((f32[96,768]{1,0:T(8,128)S(1)}, f32[96,768]{1,0:T(8,128)S(1)}, u32[]{:S(2)}, u32[]{:S(2)}) %collective-permute-start.17) | collective-permute-done | bytes 294944 | tf_op jit(solution)/shard_map/ppermute | solution.py:323
  103.3 5.3 %collective-permute-done.15 = f32[96,768]{1,0:T(8,128)S(1)} collective-permute-done((f32[96,768]{1,0:T(8,128)S(1)}, f32[96,768]{1,0:T(8,128)S(1)}, u32[]{:S(2)}, u32[]{:S(2)}) %collective-permute-start.15) | collective-permute-done | bytes 294944 | tf_op jit(solution)/shard_map/ppermute | solution.py:323
  110.8 7.9 %collective-permute-done.19.refs_3_ = f32[96,768]{1,0:T(8,128)S(1)} collective-permute-done((f32[96,768]{1,0:T(8,128)S(1)}, f32[96,768]{1,0:T(8,128)S(1)}, u32[]{:S(2)}, u32[]{:S(2)}) %collective-permute-start.19) | collective-permute-done | bytes 294944 | tf_op jit(solution)/shard_map/ppermute | solution.py:323
  118.8 4.4 %collective-permute-done.18.refs_2_ = f32[96,768]{1,0:T(8,128)S(1)} collective-permute-done((f32[96,768]{1,0:T(8,128)S(1)}, f32[96,768]{1,0:T(8,128)S(1)}, u32[]{:S(2)}, u32[]{:S(2)}) %collective-permute-start.18) | collective-permute-done | bytes 294944 | tf_op jit(solution)/shard_map/ppermute | solution.py:323
  125.3 4.9 %cols_sweep.5 = (f32[96,768]{1,0:T(8,128)S(1)}, f32[96,768]{1,0:T(8,128)S(1)}, bf16[12,384,256]{2,1,0:T(8,128)(2,1)S(1)}) custom-call(s32[9]{0:T(128)S(1)} %copy-done.14, s32[288]{0:T(512)S(1)} %get-tuple-element.99.row_of, s32[288]{0:T(512)S(1)} %select_reduce_fusion.10.col_of, s32[288]{0:T(512)S(1)} %get-tuple-element.108.strip_of, ...), custom_call_target="tpu_custom_call" | custom-call | flops 1358954496 | bytes 4718592 | tf_op jit(solution)/shard_map/cols_sweep/pallas_call | solution.py:199
  132.3 7.2 %cols_sweep.9 = (f32[96,768]{1,0:T(8,128)S(1)}, f32[96,768]{1,0:T(8,128)S(1)}, f32[96,768]{1,0:T(8,128)S(1)}, f32[96,768]{1,0:T(8,128)S(1)}) custom-call(s32[9]{0:T(128)S(1)} %copy-done.14, s32[288]{0:T(512)S(1)} %get-tuple-element.99.row_of, s32[288]{0:T(512)S(1)} %select_reduce_fusion.10.col_of, s32[288]{0:T(512)S(1)} %get-tuple-element.108.strip_of, ...), custom_call_target="tpu_custom_call" | custom-call | flops 2717908992 | bytes 9437184 | tf_op jit(solution)/shard_map/cols_sweep/pallas_call | solution.py:199
  143.8 8.1 %cols_sweep.8 = (f32[96,768]{1,0:T(8,128)S(1)}, f32[96,768]{1,0:T(8,128)S(1)}, f32[96,768]{1,0:T(8,128)S(1)}, f32[96,768]{1,0:T(8,128)S(1)}) custom-call(s32[9]{0:T(128)S(1)} %copy-done.14, s32[288]{0:T(512)S(1)} %get-tuple-element.99.row_of, s32[288]{0:T(512)S(1)} %select_reduce_fusion.10.col_of, s32[288]{0:T(512)S(1)} %get-tuple-element.108.strip_of, ...), custom_call_target="tpu_custom_call" | custom-call | flops 2717908992 | bytes 9437184 | tf_op jit(solution)/shard_map/cols_sweep/pallas_call | solution.py:199
  152.1 2.1 %collective-permute-start.27 = (f32[96,768]{1,0:T(8,128)S(1)}, f32[96,768]{1,0:T(8,128)S(1)}, u32[]{:S(2)}, u32[]{:S(2)}) collective-permute-start(f32[96,768]{1,0:T(8,128)S(1)} %add.178), channel_id=1, source_target_pairs={{2,0},{4,2},{6,4},{7,6},{5,7},{3,5},{1,3},{0,1},{10,8},{12,10},{14... | collective-permute-start | bytes 884744 | tf_op jit(solution)/shard_map/ppermute | solution.py:323
  159.5 8.7 %cols_sweep.7 = (f32[96,768]{1,0:T(8,128)S(1)}, f32[96,768]{1,0:T(8,128)S(1)}, f32[96,768]{1,0:T(8,128)S(1)}, f32[96,768]{1,0:T(8,128)S(1)}) custom-call(s32[9]{0:T(128)S(1)} %copy-done.14, s32[288]{0:T(512)S(1)} %get-tuple-element.99.row_of, s32[288]{0:T(512)S(1)} %select_reduce_fusion.10.col_of, s32[288]{0:T(512)S(1)} %get-tuple-element.108.strip_of, ...), custom_call_target="tpu_custom_call" | custom-call | flops 2717908992 | bytes 9437184 | tf_op jit(solution)/shard_map/cols_sweep/pallas_call | solution.py:199
  170.6 2.3 %collective-permute-start.25 = (f32[96,768]{1,0:T(8,128)S(1)}, f32[96,768]{1,0:T(8,128)S(1)}, u32[]{:S(2)}, u32[]{:S(2)}) collective-permute-start(f32[96,768]{1,0:T(8,128)S(1)} %add.176), channel_id=1, source_target_pairs={{0,2},{2,4},{4,6},{6,7},{7,5},{5,3},{3,1},{1,0},{8,10},{10,12},{12... | collective-permute-start | bytes 884744 | tf_op jit(solution)/shard_map/ppermute | solution.py:323
  172.9 2.5 %fusion.4 = f32[768,384]{1,0:T(8,128)} fusion(f32[96,768]{1,0:T(8,128)S(1)} %fusion.23.refs_1_, f32[96,768]{1,0:T(8,128)S(1)} %fusion.27.refs_0_, f32[384]{0:T(512)S(1)} %copy-done.20, s32[384]{0:T(512)S(1)} %copy-done.18), kind=kOutput, calls=%fused_computation.13 | convolution fusion | flops 679772160 | bytes 1772544 | tf_op jit(solution)/shard_map/dot_general | solution.py:303
  175.4 4.4 %cols_sweep.6 = (f32[96,768]{1,0:T(8,128)S(1)}, f32[96,768]{1,0:T(8,128)S(1)}) custom-call(s32[9]{0:T(128)S(1)} %copy-done.14, s32[288]{0:T(512)S(1)} %get-tuple-element.99.row_of, s32[288]{0:T(512)S(1)} %select_reduce_fusion.10.col_of, s32[288]{0:T(512)S(1)} %get-tuple-element.108.strip_of, s32[288]{0:T(512)S(1)} %get-tuple-element.98.place_of, ...), custom_call_target="tpu_custom_call" | custom-call | flops 1358954496 | bytes 4718592 | tf_op jit(solution)/shard_map/cols_sweep/pallas_call | solution.py:199
  181.8 2.5 %fusion = f32[768,384]{1,0:T(8,128)} fusion(f32[96,768]{1,0:T(8,128)S(1)} %get-tuple-element.101, f32[96,768]{1,0:T(8,128)S(1)} %get-tuple-element.100, f32[384]{0:T(512)S(1)} %copy-done.20, s32[384]{0:T(512)S(1)} %copy-done.18), kind=kOutput, calls=%fused_computation.9 | convolution fusion | flops 679772160 | bytes 1772544 | tf_op jit(solution)/shard_map/dot_general | solution.py:303
  (169 shorter events, 59.0 us)
Async XLA Ops:
  7.0 13.3 %collective-permute-start.2 = (f32[96,768]{1,0:T(8,128)S(1)}, f32[96,768]{1,0:T(8,128)S(1)}, u32[]{:S(2)}, u32[]{:S(2)}) collective-permute-start(f32[96,768]{1,0:T(8,128)S(1)} %get-tuple-element.107.refs_0_), channel_id=1, source_target_pairs={{2,0},{4,2},{6,4},{7,6},{5,7},{3,5},{1,3},{0,1},{10,8},{12,10},{14... | collective-permute-start | bytes 884744 | tf_op jit(solution)/shard_map/ppermute | solution.py:323
  7.7 12.6 %collective-permute-start.1 = (f32[96,768]{1,0:T(8,128)S(1)}, f32[96,768]{1,0:T(8,128)S(1)}, u32[]{:S(2)}, u32[]{:S(2)}) collective-permute-start(f32[96,768]{1,0:T(8,128)S(1)} %get-tuple-element.106.refs_1_), channel_id=1, source_target_pairs={{0,2},{2,4},{4,6},{6,7},{7,5},{5,3},{3,1},{1,0},{8,10},{10,12},{12... | collective-permute-start | bytes 884744 | tf_op jit(solution)/shard_map/ppermute | solution.py:323
  9.7 12.0 %collective-permute-start.3 = (f32[96,768]{1,0:T(8,128)S(1)}, f32[96,768]{1,0:T(8,128)S(1)}, u32[]{:S(2)}, u32[]{:S(2)}) collective-permute-start(f32[96,768]{1,0:T(8,128)S(1)} %get-tuple-element.106.refs_1_), channel_id=1, source_target_pairs={{2,0},{4,2},{6,4},{7,6},{5,7},{3,5},{1,3},{0,1},{10,8},{12,10},{14... | collective-permute-start | bytes 884744 | tf_op jit(solution)/shard_map/ppermute | solution.py:323
  24.1 11.8 %collective-permute-start.5 = (f32[96,768]{1,0:T(8,128)S(1)}, f32[96,768]{1,0:T(8,128)}, u32[]{:S(2)}, u32[]{:S(2)}) collective-permute-start(f32[96,768]{1,0:T(8,128)S(1)} %collective-permute-done.1.refs_1_), channel_id=1, source_target_pairs={{0,2},{2,4},{4,6},{6,7},{7,5},{5,3},{3,1},{1,0},{8,10},{10,12},{12... | collective-permute-start | bytes 884744 | tf_op jit(solution)/shard_map/ppermute | solution.py:323
  27.5 12.3 %collective-permute-start.7 = (f32[96,768]{1,0:T(8,128)S(1)}, f32[96,768]{1,0:T(8,128)}, u32[]{:S(2)}, u32[]{:S(2)}) collective-permute-start(f32[96,768]{1,0:T(8,128)S(1)} %collective-permute-done.3.refs_3_), channel_id=1, source_target_pairs={{2,0},{4,2},{6,4},{7,6},{5,7},{3,5},{1,3},{0,1},{10,8},{12,10},{14... | collective-permute-start | bytes 884744 | tf_op jit(solution)/shard_map/ppermute | solution.py:323
  39.8 25.2 %collective-permute-start.10 = (f32[96,768]{1,0:T(8,128)}, f32[96,768]{1,0:T(8,128)}, u32[]{:S(2)}, u32[]{:S(2)}) collective-permute-start(f32[96,768]{1,0:T(8,128)} %collective-permute-done.6.refs_2_), channel_id=1, source_target_pairs={{2,0},{4,2},{6,4},{7,6},{5,7},{3,5},{1,3},{0,1},{10,8},{12,10},{14... | collective-permute-start | bytes 884744 | tf_op jit(solution)/shard_map/ppermute | solution.py:323
  40.3 24.7 %collective-permute-start.11 = (f32[96,768]{1,0:T(8,128)}, f32[96,768]{1,0:T(8,128)}, u32[]{:S(2)}, u32[]{:S(2)}) collective-permute-start(f32[96,768]{1,0:T(8,128)} %collective-permute-done.7.refs_3_), channel_id=1, source_target_pairs={{2,0},{4,2},{6,4},{7,6},{5,7},{3,5},{1,3},{0,1},{10,8},{12,10},{14... | collective-permute-start | bytes 884744 | tf_op jit(solution)/shard_map/ppermute | solution.py:323
  40.7 24.3 %collective-permute-start.8 = (f32[96,768]{1,0:T(8,128)}, f32[96,768]{1,0:T(8,128)}, u32[]{:S(2)}, u32[]{:S(2)}) collective-permute-start(f32[96,768]{1,0:T(8,128)} %collective-permute-done.4.refs_0_), channel_id=1, source_target_pairs={{0,2},{2,4},{4,6},{6,7},{7,5},{5,3},{3,1},{1,0},{8,10},{10,12},{12... | collective-permute-start | bytes 884744 | tf_op jit(solution)/shard_map/ppermute | solution.py:323
  42.3 22.7 %collective-permute-start.9 = (f32[96,768]{1,0:T(8,128)}, f32[96,768]{1,0:T(8,128)}, u32[]{:S(2)}, u32[]{:S(2)}) collective-permute-start(f32[96,768]{1,0:T(8,128)} %collective-permute-done.5.refs_1_), channel_id=1, source_target_pairs={{0,2},{2,4},{4,6},{6,7},{7,5},{5,3},{3,1},{1,0},{8,10},{10,12},{12... | collective-permute-start | bytes 884744 | tf_op jit(solution)/shard_map/ppermute | solution.py:323
  65.0 20.6 %collective-permute-start.12 = (f32[96,768]{1,0:T(8,128)}, f32[96,768]{1,0:T(8,128)S(1)}, u32[]{:S(2)}, u32[]{:S(2)}) collective-permute-start(f32[96,768]{1,0:T(8,128)} %collective-permute-done.8.refs_0_), channel_id=1, source_target_pairs={{0,2},{2,4},{4,6},{6,7},{7,5},{5,3},{3,1},{1,0},{8,10},{10,12},{12... | collective-permute-start | bytes 884744 | tf_op jit(solution)/shard_map/ppermute | solution.py:323
  65.1 20.5 %collective-permute-start.13 = (f32[96,768]{1,0:T(8,128)}, f32[96,768]{1,0:T(8,128)S(1)}, u32[]{:S(2)}, u32[]{:S(2)}) collective-permute-start(f32[96,768]{1,0:T(8,128)} %collective-permute-done.11.refs_3_), channel_id=1, source_target_pairs={{2,0},{4,2},{6,4},{7,6},{5,7},{3,5},{1,3},{0,1},{10,8},{12,10},{14... | collective-permute-start | bytes 884744 | tf_op jit(solution)/shard_map/ppermute | solution.py:323
  93.8 14.8 %collective-permute-start.15 = (f32[96,768]{1,0:T(8,128)S(1)}, f32[96,768]{1,0:T(8,128)S(1)}, u32[]{:S(2)}, u32[]{:S(2)}) collective-permute-start(f32[96,768]{1,0:T(8,128)S(1)} %slice_add_fusion.3), channel_id=1, source_target_pairs={{0,16},{8,24},{16,0},{24,8},{1,17},{9,25},{17,1},{25,9},{2,18},{10... | collective-permute-start | bytes 884744 | tf_op jit(solution)/shard_map/ppermute | solution.py:323
  109.0 14.1 %collective-permute-start.18 = (f32[96,768]{1,0:T(8,128)S(1)}, f32[96,768]{1,0:T(8,128)S(1)}, u32[]{:S(2)}, u32[]{:S(2)}) collective-permute-start(f32[96,768]{1,0:T(8,128)S(1)} %fusion.27.refs_0_), channel_id=1, source_target_pairs={{0,16},{8,24},{16,0},{24,8},{1,17},{9,25},{17,1},{25,9},{2,18},{10... | collective-permute-start | bytes 884744 | tf_op jit(solution)/shard_map/ppermute | solution.py:323
  130.3 11.5 %collective-permute-start.22 = (f32[96,768]{1,0:T(8,128)S(1)}, f32[96,768]{1,0:T(8,128)S(1)}, u32[]{:S(2)}, u32[]{:S(2)}) collective-permute-start(f32[96,768]{1,0:T(8,128)S(1)} %get-tuple-element.70), channel_id=1, source_target_pairs={{0,2},{2,4},{4,6},{6,7},{7,5},{5,3},{3,1},{1,0},{8,10},{10,12},{12... | collective-permute-start | bytes 884744 | tf_op jit(solution)/shard_map/ppermute | solution.py:369
  139.5 12.4 %collective-permute-start.29 = (f32[96,768]{1,0:T(8,128)S(1)}, f32[96,768]{1,0:T(8,128)S(1)}, u32[]{:S(2)}, u32[]{:S(2)}) collective-permute-start(f32[96,768]{1,0:T(8,128)S(1)} %get-tuple-element.78), channel_id=1, source_target_pairs={{0,2},{2,4},{4,6},{6,7},{7,5},{5,3},{3,1},{1,0},{8,10},{10,12},{12... | collective-permute-start | bytes 884744 | tf_op jit(solution)/shard_map/ppermute | solution.py:323
  139.6 12.5 %collective-permute-start.26 = (f32[96,768]{1,0:T(8,128)S(1)}, f32[96,768]{1,0:T(8,128)S(1)}, u32[]{:S(2)}, u32[]{:S(2)}) collective-permute-start(f32[96,768]{1,0:T(8,128)S(1)} %get-tuple-element.73), channel_id=1, source_target_pairs={{2,0},{4,2},{6,4},{7,6},{5,7},{3,5},{1,3},{0,1},{10,8},{12,10},{14... | collective-permute-start | bytes 884744 | tf_op jit(solution)/shard_map/ppermute | solution.py:323
  141.7 14.2 %collective-permute-start.33 = (f32[96,768]{1,0:T(8,128)S(1)}, f32[96,768]{1,0:T(8,128)S(1)}, u32[]{:S(2)}, u32[]{:S(2)}) collective-permute-start(f32[96,768]{1,0:T(8,128)S(1)} %add.185), channel_id=1, source_target_pairs={{2,0},{4,2},{6,4},{7,6},{5,7},{3,5},{1,3},{0,1},{10,8},{12,10},{14... | collective-permute-start | bytes 884744 | tf_op jit(solution)/shard_map/ppermute | solution.py:323
  141.8 16.1 %collective-permute-start.23 = (f32[96,768]{1,0:T(8,128)S(1)}, f32[96,768]{1,0:T(8,128)S(1)}, u32[]{:S(2)}, u32[]{:S(2)}) collective-permute-start(f32[96,768]{1,0:T(8,128)S(1)} %add.174), channel_id=1, source_target_pairs={{0,2},{2,4},{4,6},{6,7},{7,5},{5,3},{3,1},{1,0},{8,10},{10,12},{12... | collective-permute-start | bytes 884744 | tf_op jit(solution)/shard_map/ppermute | solution.py:323
  152.0 16.2 %collective-permute-start.30 = (f32[96,768]{1,0:T(8,128)S(1)}, f32[96,768]{1,0:T(8,128)S(1)}, u32[]{:S(2)}, u32[]{:S(2)}) collective-permute-start(f32[96,768]{1,0:T(8,128)S(1)} %add.182), channel_id=1, source_target_pairs={{0,2},{2,4},{4,6},{6,7},{7,5},{5,3},{3,1},{1,0},{8,10},{10,12},{12... | collective-permute-start | bytes 884744 | tf_op jit(solution)/shard_map/ppermute | solution.py:323
  152.1 16.2 %collective-permute-start.27 = (f32[96,768]{1,0:T(8,128)S(1)}, f32[96,768]{1,0:T(8,128)S(1)}, u32[]{:S(2)}, u32[]{:S(2)}) collective-permute-start(f32[96,768]{1,0:T(8,128)S(1)} %add.178), channel_id=1, source_target_pairs={{2,0},{4,2},{6,4},{7,6},{5,7},{3,5},{1,3},{0,1},{10,8},{12,10},{14... | collective-permute-start | bytes 884744 | tf_op jit(solution)/shard_map/ppermute | solution.py:323
  155.9 14.6 %collective-permute-start.34 = (f32[96,768]{1,0:T(8,128)S(1)}, f32[96,768]{1,0:T(8,128)S(1)}, u32[]{:S(2)}, u32[]{:S(2)}) collective-permute-start(f32[96,768]{1,0:T(8,128)S(1)} %add.186), channel_id=1, source_target_pairs={{2,0},{4,2},{6,4},{7,6},{5,7},{3,5},{1,3},{0,1},{10,8},{12,10},{14... | collective-permute-start | bytes 884744 | tf_op jit(solution)/shard_map/ppermute | solution.py:323
  158.0 12.6 %collective-permute-start.24 = (f32[96,768]{1,0:T(8,128)S(1)}, f32[96,768]{1,0:T(8,128)S(1)}, u32[]{:S(2)}, u32[]{:S(2)}) collective-permute-start(f32[96,768]{1,0:T(8,128)S(1)} %add.175), channel_id=1, source_target_pairs={{0,2},{2,4},{4,6},{6,7},{7,5},{5,3},{3,1},{1,0},{8,10},{10,12},{12... | collective-permute-start | bytes 884744 | tf_op jit(solution)/shard_map/ppermute | solution.py:323
  168.3 11.6 %collective-permute-start.31 = (f32[96,768]{1,0:T(8,128)S(1)}, f32[96,768]{1,0:T(8,128)S(1)}, u32[]{:S(2)}, u32[]{:S(2)}) collective-permute-start(f32[96,768]{1,0:T(8,128)S(1)} %add.183), channel_id=1, source_target_pairs={{0,2},{2,4},{4,6},{6,7},{7,5},{5,3},{3,1},{1,0},{8,10},{10,12},{12... | collective-permute-start | bytes 884744 | tf_op jit(solution)/shard_map/ppermute | solution.py:323
  168.4 11.5 %collective-permute-start.28 = (f32[96,768]{1,0:T(8,128)S(1)}, f32[96,768]{1,0:T(8,128)S(1)}, u32[]{:S(2)}, u32[]{:S(2)}) collective-permute-start(f32[96,768]{1,0:T(8,128)S(1)} %add.179), channel_id=1, source_target_pairs={{2,0},{4,2},{6,4},{7,6},{5,7},{3,5},{1,3},{0,1},{10,8},{12,10},{14... | collective-permute-start | bytes 884744 | tf_op jit(solution)/shard_map/ppermute | solution.py:323
  (41 other events, 218.4 us)

commit v3 on v2

--- a/solution.py
+++ b/solution.py
@@ -326,11 +326,13 @@
         return cut(vir_energies(index, eps_vir, offset, fine)[None, :] - occ_pair[:, None])
 
     near = n_res // 2
-    own = cut(compact(amplitudes))
-    first_other, second_other = compact(other_first), compact(other_second)
+    own = [compact(amplitudes)]
+    first_other = compact(other_first)
     ahead = behind = own
     ladder = rows_sweep((0, 1), strip_tiles, integrals, [own], rows)
     for s in range(1, near):
+        if s == near - 1:
+            ahead, behind = cut(ahead[0]), cut(behind[0])
         ahead, behind = send(ahead, "res", onward), send(behind, "res", backward)
         ahead, behind = lax.optimization_barrier((ahead, behind))
         ladder = rows_sweep((2 * s - 1, 2 * s + 1), strip_tiles, integrals, [ahead, behind], rows, ladder)
@@ -341,7 +343,7 @@
     bit = 1
     while bit < n_con:
         swap = [(i, i ^ bit) for i in range(n_con)]
-        came = send(sent, "con", swap)
+        came = send(sent[:-1], "con", swap) + send(sent[-1:], "con", swap)
         bit *= 2
         if bit < n_con:
             mid = kept[0].shape[1] // 2
@@ -365,6 +367,8 @@
         block = [jnp.concatenate([h[p] for h in held], axis=1) if len(held) > 1 else held[0][p] for p in parts]
         held = held + [send(block[:-1], "con", swap) + send(block[-1:], "con", swap)]
     first_out = expand(jnp.concatenate(firsts, axis=0))
+    late_other, _ = lax.optimization_barrier((other_second, firsts[-1]))
+    second_other = cut(compact(late_other))
     *far, split = cols_sweep((n_res - 1, n_res), strip_tiles, integrals, held, fine, pieces=1, keeps=True)
     ahead = [lax.ppermute(far[p], "res", onward) if p < PARTS // 2 else None for p in parts]
     behind = [None if p < PARTS // 2 else lax.ppermute(far[p], "res", backward) for p in parts]
@@ -375,7 +379,6 @@
         ahead = send([to_ahead[p] if ahead[p] is None else to_ahead[p] + ahead[p] for p in parts], "res", onward)
         behind = send([to_behind[p] if behind[p] is None else to_behind[p] + behind[p] for p in parts], "res", backward)
     mine = cols_sweep((0, 1), strip_tiles, integrals, None, fine, pieces=1, split=split)
-    second_other = cut(second_other)
     seconds = [
         (0.5 * second_other[p] + ((mine[p] + ahead[p]) + behind[p])) / second_scale[p] for p in parts
     ]

time: 185 us -> 180 us (0.973)
  local copies, waits for them, and re-layouts: 12.1 us -> 7.31 us
  starting transfers between devices: 34.9 us -> 30.8 us
  other arithmetic: 8.7 us -> 12.6 us
    unnamed x58 -> x50, local copies, waits for them, and re-layouts: 10.8 us -> 3.72 us
    ppermute x34 -> x30, starting transfers between devices: 32.8 us -> 28.8 us  [send(): return [lax.ppermute(value, axis, perm) for value in values]]
    ppermute x34 -> x30, waiting for transfers between devices: 46.1 us -> 45.7 us  [send(): return [lax.ppermute(value, axis, perm) for value in values]]
  transfers between devices with their start and end apart: 36 -> 32, of which waited for: 15 -> 12; matrix products, arithmetic and copies ran while one was open for 7% -> 11% of each run, Pallas kernels for 33% -> 34%
where the time goes in v3:
time: 180 us; the launch traced here: 179 us
  Pallas kernels  71 us (39%)
  waiting for transfers between devices  45.7 us (25%)
  starting transfers between devices  30.8 us (17%)
  other arithmetic  12.6 us (7%)
  matrix products  10.3 us (6%)
  local copies, waits for them, and re-layouts  7.31 us (4%)
    pallas_call x10, Pallas kernels, sweep(): pl.pallas_call(functools.partial(sweep_kernel, by_rows, blocks, n_parts,...  71 us
    ppermute x30, waiting for transfers between devices, send(): return [lax.ppermute(value, axis, perm) for value in values]  45.7 us
    ppermute x30, starting transfers between devices, send(): return [lax.ppermute(value, axis, perm) for value in values]  28.8 us
    dot_general x2, matrix products, expand(): lax.dot_general(value, signed, (((0,), (0,)), ((), ())), precision=precis...  5.06 us
    dot_general x3, matrix products, compact(): lax.dot_general(signed, value, (((1,), (1,)), ((), ())), precision=precis...  4.29 us
    unnamed x50, local copies, waits for them, and re-layouts  3.72 us
  transfers between devices with their start and end apart: 32, of which 12 were waited for; matrix products, arithmetic and copies ran while one was open for 11% of the time, Pallas kernels for 34%

profile of v3, /device:TPU:0, one launch (start us, length us, event | category | flops | bytes accessed | tf_op | source)
XLA Modules:
  0.0 179.0 jit_solution(11014118935474430177)
XLA Ops:
  3.8 3.1 %collective-permute-start = (f32[192,768]{1,0:T(8,128)S(1)}, f32[192,768]{1,0:T(8,128)S(1)}, u32[]{:S(2)}, u32[]{:S(2)}) collective-permute-start(f32[192,768]{1,0:T(8,128)S(1)} %fusion.8.refs_0_), channel_id=1, source_target_pairs={{0,2},{2,4},{4,6},{6,7},{7,5},{5,3},{3,1},{1,0},{8,10},{10,12},{12... | collective-permute-start | bytes 1769480 | tf_op jit(solution)/shard_map/ppermute | solution.py:323
  13.1 7.0 %collective-permute-done.refs_0_ = f32[192,768]{1,0:T(8,128)S(1)} collective-permute-done((f32[192,768]{1,0:T(8,128)S(1)}, f32[192,768]{1,0:T(8,128)S(1)}, u32[]{:S(2)}, u32[]{:S(2)}) %collective-permute-start) | collective-permute-done | bytes 589856 | tf_op jit(solution)/shard_map/ppermute | solution.py:323
  26.1 9.5 %collective-permute-done.2.refs_0_ = f32[192,768]{1,0:T(8,128)S(1)} collective-permute-done((f32[192,768]{1,0:T(8,128)S(1)}, f32[192,768]{1,0:T(8,128)S(1)}, u32[]{:S(2)}, u32[]{:S(2)}) %collective-permute-start.2) | collective-permute-done | bytes 589856 | tf_op jit(solution)/shard_map/ppermute | solution.py:323
  42.8 5.0 %rows_sweep.5.refs_2_ = f32[192,3072]{1,0:T(8,128)S(1)} custom-call(s32[9]{0:T(128)S(1)} %select_reduce_fusion.11.starts, s32[288]{0:T(512)S(1)} %get-tuple-element.93.row_of, s32[288]{0:T(512)S(1)} %select_reduce_fusion.10.col_of, s32[288]{0:T(512)S(1)} %get-tuple-element.104.strip_of, s32[288]{0:T(512)S(1)} %get-tuple-element.92.place_of, ...), custom_call_target="tpu_custom_call" | custom-call | flops 1358954496 | bytes 4718592 | tf_op jit(solution)/shard_map/rows_sweep/pallas_call | solution.py:199
  50.6 9.7 %rows_sweep.6.refs_2_ = f32[192,3072]{1,0:T(8,128)S(1)} custom-call(s32[9]{0:T(128)S(1)} %copy-done.12, s32[288]{0:T(512)S(1)} %get-tuple-element.93.row_of, s32[288]{0:T(512)S(1)} %select_reduce_fusion.10.col_of, s32[288]{0:T(512)S(1)} %get-tuple-element.104.strip_of, s32[288]{0:T(512)S(1)} %get-tuple-element.92.place_of, ...), custom_call_target="tpu_custom_call", output_to_operand_aliasing={{}: (8, {})} | custom-call | flops 2717908992 | bytes 9437184 | tf_op jit(solution)/shard_map/rows_sweep/pallas_call | solution.py:199
  62.4 9.0 %rows_sweep.7.refs_4_ = f32[192,3072]{1,0:T(8,128)S(1)} custom-call(s32[9]{0:T(128)S(1)} %copy-done.12, s32[288]{0:T(512)S(1)} %get-tuple-element.93.row_of, s32[288]{0:T(512)S(1)} %select_reduce_fusion.10.col_of, s32[288]{0:T(512)S(1)} %get-tuple-element.104.strip_of, s32[288]{0:T(512)S(1)} %get-tuple-element.92.place_of, ...), custom_call_target="tpu_custom_call", output_to_operand_aliasing={{}: (8, {})} | custom-call | flops 2717908992 | bytes 9437184 | tf_op jit(solution)/shard_map/rows_sweep/pallas_call | solution.py:199
  71.4 8.7 %rows_sweep.8.refs_2_ = f32[192,3072]{1,0:T(8,128)S(1)} custom-call(s32[9]{0:T(128)S(1)} %copy-done.12, s32[288]{0:T(512)S(1)} %get-tuple-element.93.row_of, s32[288]{0:T(512)S(1)} %select_reduce_fusion.10.col_of, s32[288]{0:T(512)S(1)} %get-tuple-element.104.strip_of, s32[288]{0:T(512)S(1)} %get-tuple-element.92.place_of, ...), custom_call_target="tpu_custom_call", output_to_operand_aliasing={{}: (10, {})} | custom-call | flops 2717908992 | bytes 9437184 | tf_op jit(solution)/shard_map/rows_sweep/pallas_call | solution.py:199
  80.2 5.2 %rows_sweep.9 = (f32[96,1536]{1,0:T(8,128)S(1)}, f32[96,1536]{1,0:T(8,128)S(1)}, f32[96,1536]{1,0:T(8,128)S(1)}, f32[96,1536]{1,0:T(8,128)S(1)}) custom-call(s32[9]{0:T(128)S(1)} %copy-done.12, s32[288]{0:T(512)S(1)} %get-tuple-element.93.row_of, s32[288]{0:T(512)S(1)} %select_reduce_fusion.10.col_of, s32[288]{0:T(512)S(1)} %get-tuple-element.104.strip_of, ...), custom_call_target="tpu_custom_call" | custom-call | flops 1358954496 | bytes 4718592 | tf_op jit(solution)/shard_map/rows_sweep/pallas_call | solution.py:199
  91.0 3.5 %select_reduce_fusion = (f32[768]{0:T(1024)S(1)}, f32[768]{0:T(1024)S(1)}, f32[768]{0:T(1024)S(1)}, f32[768]{0:T(1024)S(1)}) fusion(s32[768]{0:T(1024)S(1)} %get-tuple-element.78, f32[1600]{0:T(1024)S(1)} %copy-done.24, s32[768]{0:T(1024)S(1)} %get-tuple-element.81, s32[768]{0:T(1024)S(1)} %get-tuple-element.79, s32[768]{0:T(1024)S(1)} %get-tuple-element.80), kind=kLoop, calls=%fused_computation | loop fusion | flops 14742528 | bytes 30976 | tf_op jit(solution)/shard_map/reduce_sum | solution.py:271
  94.8 3.0 %collective-permute-done.13 = f32[96,768]{1,0:T(8,128)S(1)} collective-permute-done((f32[96,768]{1,0:T(8,128)S(1)}, f32[96,768]{1,0:T(8,128)S(1)}, u32[]{:S(2)}, u32[]{:S(2)}) %collective-permute-start.13) | collective-permute-done | bytes 294944 | tf_op jit(solution)/shard_map/ppermute | solution.py:323
  97.9 5.3 %collective-permute-done.11 = f32[96,768]{1,0:T(8,128)S(1)} collective-permute-done((f32[96,768]{1,0:T(8,128)S(1)}, f32[96,768]{1,0:T(8,128)S(1)}, u32[]{:S(2)}, u32[]{:S(2)}) %collective-permute-start.11) | collective-permute-done | bytes 294944 | tf_op jit(solution)/shard_map/ppermute | solution.py:323
  105.4 7.9 %collective-permute-done.15.refs_3_ = f32[96,768]{1,0:T(8,128)S(1)} collective-permute-done((f32[96,768]{1,0:T(8,128)S(1)}, f32[96,768]{1,0:T(8,128)S(1)}, u32[]{:S(2)}, u32[]{:S(2)}) %collective-permute-start.15) | collective-permute-done | bytes 294944 | tf_op jit(solution)/shard_map/ppermute | solution.py:323
  113.4 4.4 %collective-permute-done.14.refs_2_ = f32[96,768]{1,0:T(8,128)S(1)} collective-permute-done((f32[96,768]{1,0:T(8,128)S(1)}, f32[96,768]{1,0:T(8,128)S(1)}, u32[]{:S(2)}, u32[]{:S(2)}) %collective-permute-start.14) | collective-permute-done | bytes 294944 | tf_op jit(solution)/shard_map/ppermute | solution.py:323
  119.9 4.9 %cols_sweep.5 = (f32[96,768]{1,0:T(8,128)S(1)}, f32[96,768]{1,0:T(8,128)S(1)}, bf16[12,384,256]{2,1,0:T(8,128)(2,1)S(1)}) custom-call(s32[9]{0:T(128)S(1)} %copy-done.12, s32[288]{0:T(512)S(1)} %get-tuple-element.93.row_of, s32[288]{0:T(512)S(1)} %select_reduce_fusion.10.col_of, s32[288]{0:T(512)S(1)} %get-tuple-element.104.strip_of, ...), custom_call_target="tpu_custom_call" | custom-call | flops 1358954496 | bytes 4718592 | tf_op jit(solution)/shard_map/cols_sweep/pallas_call | solution.py:199
  126.9 7.2 %cols_sweep.9 = (f32[96,768]{1,0:T(8,128)S(1)}, f32[96,768]{1,0:T(8,128)S(1)}, f32[96,768]{1,0:T(8,128)S(1)}, f32[96,768]{1,0:T(8,128)S(1)}) custom-call(s32[9]{0:T(128)S(1)} %copy-done.12, s32[288]{0:T(512)S(1)} %get-tuple-element.93.row_of, s32[288]{0:T(512)S(1)} %select_reduce_fusion.10.col_of, s32[288]{0:T(512)S(1)} %get-tuple-element.104.strip_of, ...), custom_call_target="tpu_custom_call" | custom-call | flops 2717908992 | bytes 9437184 | tf_op jit(solution)/shard_map/cols_sweep/pallas_call | solution.py:199
  136.4 2.1 %collective-permute-start.19 = (f32[96,768]{1,0:T(8,128)S(1)}, f32[96,768]{1,0:T(8,128)S(1)}, u32[]{:S(2)}, u32[]{:S(2)}) collective-permute-start(f32[96,768]{1,0:T(8,128)S(1)} %add.174), channel_id=1, source_target_pairs={{0,2},{2,4},{4,6},{6,7},{7,5},{5,3},{3,1},{1,0},{8,10},{10,12},{12... | collective-permute-start | bytes 884744 | tf_op jit(solution)/shard_map/ppermute | solution.py:323
  138.5 8.1 %cols_sweep.8 = (f32[96,768]{1,0:T(8,128)S(1)}, f32[96,768]{1,0:T(8,128)S(1)}, f32[96,768]{1,0:T(8,128)S(1)}, f32[96,768]{1,0:T(8,128)S(1)}) custom-call(s32[9]{0:T(128)S(1)} %copy-done.12, s32[288]{0:T(512)S(1)} %get-tuple-element.93.row_of, s32[288]{0:T(512)S(1)} %select_reduce_fusion.10.col_of, s32[288]{0:T(512)S(1)} %get-tuple-element.104.strip_of, ...), custom_call_target="tpu_custom_call" | custom-call | flops 2717908992 | bytes 9437184 | tf_op jit(solution)/shard_map/cols_sweep/pallas_call | solution.py:199
  146.8 2.1 %collective-permute-start.23 = (f32[96,768]{1,0:T(8,128)S(1)}, f32[96,768]{1,0:T(8,128)S(1)}, u32[]{:S(2)}, u32[]{:S(2)}) collective-permute-start(f32[96,768]{1,0:T(8,128)S(1)} %add.178), channel_id=1, source_target_pairs={{2,0},{4,2},{6,4},{7,6},{5,7},{3,5},{1,3},{0,1},{10,8},{12,10},{14... | collective-permute-start | bytes 884744 | tf_op jit(solution)/shard_map/ppermute | solution.py:323
  154.2 8.7 %cols_sweep.7 = (f32[96,768]{1,0:T(8,128)S(1)}, f32[96,768]{1,0:T(8,128)S(1)}, f32[96,768]{1,0:T(8,128)S(1)}, f32[96,768]{1,0:T(8,128)S(1)}) custom-call(s32[9]{0:T(128)S(1)} %copy-done.12, s32[288]{0:T(512)S(1)} %get-tuple-element.93.row_of, s32[288]{0:T(512)S(1)} %select_reduce_fusion.10.col_of, s32[288]{0:T(512)S(1)} %get-tuple-element.104.strip_of, ...), custom_call_target="tpu_custom_call" | custom-call | flops 2717908992 | bytes 9437184 | tf_op jit(solution)/shard_map/cols_sweep/pallas_call | solution.py:199
  163.1 2.1 %collective-permute-start.24 = (f32[96,768]{1,0:T(8,128)S(1)}, f32[96,768]{1,0:T(8,128)S(1)}, u32[]{:S(2)}, u32[]{:S(2)}) collective-permute-start(f32[96,768]{1,0:T(8,128)S(1)} %add.179), channel_id=1, source_target_pairs={{2,0},{4,2},{6,4},{7,6},{5,7},{3,5},{1,3},{0,1},{10,8},{12,10},{14... | collective-permute-start | bytes 884744 | tf_op jit(solution)/shard_map/ppermute | solution.py:323
  165.3 2.3 %collective-permute-start.21 = (f32[96,768]{1,0:T(8,128)S(1)}, f32[96,768]{1,0:T(8,128)S(1)}, u32[]{:S(2)}, u32[]{:S(2)}) collective-permute-start(f32[96,768]{1,0:T(8,128)S(1)} %add.176), channel_id=1, source_target_pairs={{0,2},{2,4},{4,6},{6,7},{7,5},{5,3},{3,1},{1,0},{8,10},{10,12},{12... | collective-permute-start | bytes 884744 | tf_op jit(solution)/shard_map/ppermute | solution.py:323
  167.6 2.5 %fusion.4 = f32[768,384]{1,0:T(8,128)} fusion(f32[96,768]{1,0:T(8,128)S(1)} %fusion.23.refs_1_, f32[96,768]{1,0:T(8,128)S(1)} %fusion.27.refs_0_, f32[384]{0:T(512)S(1)} %copy-done.18, s32[384]{0:T(512)S(1)} %copy-done.16), kind=kOutput, calls=%fused_computation.13 | convolution fusion | flops 679772160 | bytes 1772544 | tf_op jit(solution)/shard_map/dot_general | solution.py:303
  170.1 4.4 %cols_sweep.6 = (f32[96,768]{1,0:T(8,128)S(1)}, f32[96,768]{1,0:T(8,128)S(1)}) custom-call(s32[9]{0:T(128)S(1)} %copy-done.12, s32[288]{0:T(512)S(1)} %get-tuple-element.93.row_of, s32[288]{0:T(512)S(1)} %select_reduce_fusion.10.col_of, s32[288]{0:T(512)S(1)} %get-tuple-element.104.strip_of, s32[288]{0:T(512)S(1)} %get-tuple-element.92.place_of, ...), custom_call_target="tpu_custom_call" | custom-call | flops 1358954496 | bytes 4718592 | tf_op jit(solution)/shard_map/cols_sweep/pallas_call | solution.py:199
  176.5 2.5 %fusion = f32[768,384]{1,0:T(8,128)} fusion(f32[96,768]{1,0:T(8,128)S(1)} %get-tuple-element.95, f32[96,768]{1,0:T(8,128)S(1)} %get-tuple-element.94, f32[384]{0:T(512)S(1)} %copy-done.18, s32[384]{0:T(512)S(1)} %copy-done.16), kind=kOutput, calls=%fused_computation.9 | convolution fusion | flops 679772160 | bytes 1772544 | tf_op jit(solution)/shard_map/dot_general | solution.py:303
  (154 shorter events, 49.5 us)
Async XLA Ops:
  3.8 16.4 %collective-permute-start = (f32[192,768]{1,0:T(8,128)S(1)}, f32[192,768]{1,0:T(8,128)S(1)}, u32[]{:S(2)}, u32[]{:S(2)}) collective-permute-start(f32[192,768]{1,0:T(8,128)S(1)} %fusion.8.refs_0_), channel_id=1, source_target_pairs={{0,2},{2,4},{4,6},{6,7},{7,5},{5,3},{3,1},{1,0},{8,10},{10,12},{12... | collective-permute-start | bytes 1769480 | tf_op jit(solution)/shard_map/ppermute | solution.py:323
  6.9 14.8 %collective-permute-start.1 = (f32[192,768]{1,0:T(8,128)S(1)}, f32[192,768]{1,0:T(8,128)S(1)}, u32[]{:S(2)}, u32[]{:S(2)}) collective-permute-start(f32[192,768]{1,0:T(8,128)S(1)} %fusion.8.refs_0_), channel_id=1, source_target_pairs={{2,0},{4,2},{6,4},{7,6},{5,7},{3,5},{1,3},{0,1},{10,8},{12,10},{14... | collective-permute-start | bytes 1769480 | tf_op jit(solution)/shard_map/ppermute | solution.py:323
  21.7 13.9 %collective-permute-start.2 = (f32[192,768]{1,0:T(8,128)S(1)}, f32[192,768]{1,0:T(8,128)S(1)}, u32[]{:S(2)}, u32[]{:S(2)}) collective-permute-start(f32[192,768]{1,0:T(8,128)S(1)} %collective-permute-done.refs_0_), channel_id=1, source_target_pairs={{0,2},{2,4},{4,6},{6,7},{7,5},{5,3},{3,1},{1,0},{8,10},{10,12},{12... | collective-permute-start | bytes 1769480 | tf_op jit(solution)/shard_map/ppermute | solution.py:323
  23.3 13.6 %collective-permute-start.3 = (f32[192,768]{1,0:T(8,128)S(1)}, f32[192,768]{1,0:T(8,128)S(1)}, u32[]{:S(2)}, u32[]{:S(2)}) collective-permute-start(f32[192,768]{1,0:T(8,128)S(1)} %collective-permute-done.1.refs_1_), channel_id=1, source_target_pairs={{2,0},{4,2},{6,4},{7,6},{5,7},{3,5},{1,3},{0,1},{10,8},{12,10},{14... | collective-permute-start | bytes 1769480 | tf_op jit(solution)/shard_map/ppermute | solution.py:323
  37.9 22.4 %collective-permute-start.4 = (f32[96,768]{1,0:T(8,128)}, f32[96,768]{1,0:T(8,128)}, u32[]{:S(2)}, u32[]{:S(2)}) collective-permute-start(f32[96,768]{1,0:T(8,128)} %get-tuple-element.103), channel_id=1, source_target_pairs={{0,2},{2,4},{4,6},{6,7},{7,5},{5,3},{3,1},{1,0},{8,10},{10,12},{12... | collective-permute-start | bytes 884744 | tf_op jit(solution)/shard_map/ppermute | solution.py:323
  39.4 20.8 %collective-permute-start.5 = (f32[96,768]{1,0:T(8,128)}, f32[96,768]{1,0:T(8,128)}, u32[]{:S(2)}, u32[]{:S(2)}) collective-permute-start(f32[96,768]{1,0:T(8,128)} %get-tuple-element.102), channel_id=1, source_target_pairs={{0,2},{2,4},{4,6},{6,7},{7,5},{5,3},{3,1},{1,0},{8,10},{10,12},{12... | collective-permute-start | bytes 884744 | tf_op jit(solution)/shard_map/ppermute | solution.py:323
  41.8 18.5 %collective-permute-start.6 = (f32[96,768]{1,0:T(8,128)}, f32[96,768]{1,0:T(8,128)}, u32[]{:S(2)}, u32[]{:S(2)}) collective-permute-start(f32[96,768]{1,0:T(8,128)} %get-tuple-element.101), channel_id=1, source_target_pairs={{2,0},{4,2},{6,4},{7,6},{5,7},{3,5},{1,3},{0,1},{10,8},{12,10},{14... | collective-permute-start | bytes 884744 | tf_op jit(solution)/shard_map/ppermute | solution.py:323
  42.3 18.0 %collective-permute-start.7 = (f32[96,768]{1,0:T(8,128)}, f32[96,768]{1,0:T(8,128)}, u32[]{:S(2)}, u32[]{:S(2)}) collective-permute-start(f32[96,768]{1,0:T(8,128)} %get-tuple-element.100), channel_id=1, source_target_pairs={{2,0},{4,2},{6,4},{7,6},{5,7},{3,5},{1,3},{0,1},{10,8},{12,10},{14... | collective-permute-start | bytes 884744 | tf_op jit(solution)/shard_map/ppermute | solution.py:323
  60.3 19.9 %collective-permute-start.8 = (f32[96,768]{1,0:T(8,128)}, f32[96,768]{1,0:T(8,128)S(1)}, u32[]{:S(2)}, u32[]{:S(2)}) collective-permute-start(f32[96,768]{1,0:T(8,128)} %collective-permute-done.4.refs_0_), channel_id=1, source_target_pairs={{0,2},{2,4},{4,6},{6,7},{7,5},{5,3},{3,1},{1,0},{8,10},{10,12},{12... | collective-permute-start | bytes 884744 | tf_op jit(solution)/shard_map/ppermute | solution.py:323
  60.4 19.9 %collective-permute-start.9 = (f32[96,768]{1,0:T(8,128)}, f32[96,768]{1,0:T(8,128)S(1)}, u32[]{:S(2)}, u32[]{:S(2)}) collective-permute-start(f32[96,768]{1,0:T(8,128)} %collective-permute-done.7.refs_3_), channel_id=1, source_target_pairs={{2,0},{4,2},{6,4},{7,6},{5,7},{3,5},{1,3},{0,1},{10,8},{12,10},{14... | collective-permute-start | bytes 884744 | tf_op jit(solution)/shard_map/ppermute | solution.py:323
  88.4 14.8 %collective-permute-start.11 = (f32[96,768]{1,0:T(8,128)S(1)}, f32[96,768]{1,0:T(8,128)S(1)}, u32[]{:S(2)}, u32[]{:S(2)}) collective-permute-start(f32[96,768]{1,0:T(8,128)S(1)} %slice_add_fusion.3), channel_id=1, source_target_pairs={{0,16},{8,24},{16,0},{24,8},{1,17},{9,25},{17,1},{25,9},{2,18},{10... | collective-permute-start | bytes 884744 | tf_op jit(solution)/shard_map/ppermute | solution.py:323
  103.7 14.1 %collective-permute-start.14 = (f32[96,768]{1,0:T(8,128)S(1)}, f32[96,768]{1,0:T(8,128)S(1)}, u32[]{:S(2)}, u32[]{:S(2)}) collective-permute-start(f32[96,768]{1,0:T(8,128)S(1)} %fusion.27.refs_0_), channel_id=1, source_target_pairs={{0,16},{8,24},{16,0},{24,8},{1,17},{9,25},{17,1},{25,9},{2,18},{10... | collective-permute-start | bytes 884744 | tf_op jit(solution)/shard_map/ppermute | solution.py:323
  124.8 11.4 %collective-permute-start.28 = (f32[96,768]{1,0:T(8,128)S(1)}, f32[96,768]{1,0:T(8,128)S(1)}, u32[]{:S(2)}, u32[]{:S(2)}) collective-permute-start(f32[96,768]{1,0:T(8,128)S(1)} %get-tuple-element.76), channel_id=1, source_target_pairs={{2,0},{4,2},{6,4},{7,6},{5,7},{3,5},{1,3},{0,1},{10,8},{12,10},{14... | collective-permute-start | bytes 884744 | tf_op jit(solution)/shard_map/ppermute | solution.py:374
  124.9 11.5 %collective-permute-start.18 = (f32[96,768]{1,0:T(8,128)S(1)}, f32[96,768]{1,0:T(8,128)S(1)}, u32[]{:S(2)}, u32[]{:S(2)}) collective-permute-start(f32[96,768]{1,0:T(8,128)S(1)} %get-tuple-element.64), channel_id=1, source_target_pairs={{0,2},{2,4},{4,6},{6,7},{7,5},{5,3},{3,1},{1,0},{8,10},{10,12},{12... | collective-permute-start | bytes 884744 | tf_op jit(solution)/shard_map/ppermute | solution.py:373
  134.2 12.4 %collective-permute-start.25 = (f32[96,768]{1,0:T(8,128)S(1)}, f32[96,768]{1,0:T(8,128)S(1)}, u32[]{:S(2)}, u32[]{:S(2)}) collective-permute-start(f32[96,768]{1,0:T(8,128)S(1)} %get-tuple-element.72), channel_id=1, source_target_pairs={{0,2},{2,4},{4,6},{6,7},{7,5},{5,3},{3,1},{1,0},{8,10},{10,12},{12... | collective-permute-start | bytes 884744 | tf_op jit(solution)/shard_map/ppermute | solution.py:323
  134.2 12.5 %collective-permute-start.22 = (f32[96,768]{1,0:T(8,128)S(1)}, f32[96,768]{1,0:T(8,128)S(1)}, u32[]{:S(2)}, u32[]{:S(2)}) collective-permute-start(f32[96,768]{1,0:T(8,128)S(1)} %get-tuple-element.67), channel_id=1, source_target_pairs={{2,0},{4,2},{6,4},{7,6},{5,7},{3,5},{1,3},{0,1},{10,8},{12,10},{14... | collective-permute-start | bytes 884744 | tf_op jit(solution)/shard_map/ppermute | solution.py:323
  136.3 14.2 %collective-permute-start.29 = (f32[96,768]{1,0:T(8,128)S(1)}, f32[96,768]{1,0:T(8,128)S(1)}, u32[]{:S(2)}, u32[]{:S(2)}) collective-permute-start(f32[96,768]{1,0:T(8,128)S(1)} %add.185), channel_id=1, source_target_pairs={{2,0},{4,2},{6,4},{7,6},{5,7},{3,5},{1,3},{0,1},{10,8},{12,10},{14... | collective-permute-start | bytes 884744 | tf_op jit(solution)/shard_map/ppermute | solution.py:323
  136.4 16.1 %collective-permute-start.19 = (f32[96,768]{1,0:T(8,128)S(1)}, f32[96,768]{1,0:T(8,128)S(1)}, u32[]{:S(2)}, u32[]{:S(2)}) collective-permute-start(f32[96,768]{1,0:T(8,128)S(1)} %add.174), channel_id=1, source_target_pairs={{0,2},{2,4},{4,6},{6,7},{7,5},{5,3},{3,1},{1,0},{8,10},{10,12},{12... | collective-permute-start | bytes 884744 | tf_op jit(solution)/shard_map/ppermute | solution.py:323
  146.6 16.3 %collective-permute-start.26 = (f32[96,768]{1,0:T(8,128)S(1)}, f32[96,768]{1,0:T(8,128)S(1)}, u32[]{:S(2)}, u32[]{:S(2)}) collective-permute-start(f32[96,768]{1,0:T(8,128)S(1)} %add.182), channel_id=1, source_target_pairs={{0,2},{2,4},{4,6},{6,7},{7,5},{5,3},{3,1},{1,0},{8,10},{10,12},{12... | collective-permute-start | bytes 884744 | tf_op jit(solution)/shard_map/ppermute | solution.py:323
  146.8 16.3 %collective-permute-start.23 = (f32[96,768]{1,0:T(8,128)S(1)}, f32[96,768]{1,0:T(8,128)S(1)}, u32[]{:S(2)}, u32[]{:S(2)}) collective-permute-start(f32[96,768]{1,0:T(8,128)S(1)} %add.178), channel_id=1, source_target_pairs={{2,0},{4,2},{6,4},{7,6},{5,7},{3,5},{1,3},{0,1},{10,8},{12,10},{14... | collective-permute-start | bytes 884744 | tf_op jit(solution)/shard_map/ppermute | solution.py:323
  150.5 14.6 %collective-permute-start.30 = (f32[96,768]{1,0:T(8,128)S(1)}, f32[96,768]{1,0:T(8,128)S(1)}, u32[]{:S(2)}, u32[]{:S(2)}) collective-permute-start(f32[96,768]{1,0:T(8,128)S(1)} %add.186), channel_id=1, source_target_pairs={{2,0},{4,2},{6,4},{7,6},{5,7},{3,5},{1,3},{0,1},{10,8},{12,10},{14... | collective-permute-start | bytes 884744 | tf_op jit(solution)/shard_map/ppermute | solution.py:323
  152.6 12.7 %collective-permute-start.20 = (f32[96,768]{1,0:T(8,128)S(1)}, f32[96,768]{1,0:T(8,128)S(1)}, u32[]{:S(2)}, u32[]{:S(2)}) collective-permute-start(f32[96,768]{1,0:T(8,128)S(1)} %add.175), channel_id=1, source_target_pairs={{0,2},{2,4},{4,6},{6,7},{7,5},{5,3},{3,1},{1,0},{8,10},{10,12},{12... | collective-permute-start | bytes 884744 | tf_op jit(solution)/shard_map/ppermute | solution.py:323
  163.0 11.6 %collective-permute-start.27 = (f32[96,768]{1,0:T(8,128)S(1)}, f32[96,768]{1,0:T(8,128)S(1)}, u32[]{:S(2)}, u32[]{:S(2)}) collective-permute-start(f32[96,768]{1,0:T(8,128)S(1)} %add.183), channel_id=1, source_target_pairs={{0,2},{2,4},{4,6},{6,7},{7,5},{5,3},{3,1},{1,0},{8,10},{10,12},{12... | collective-permute-start | bytes 884744 | tf_op jit(solution)/shard_map/ppermute | solution.py:323
  163.1 11.5 %collective-permute-start.24 = (f32[96,768]{1,0:T(8,128)S(1)}, f32[96,768]{1,0:T(8,128)S(1)}, u32[]{:S(2)}, u32[]{:S(2)}) collective-permute-start(f32[96,768]{1,0:T(8,128)S(1)} %add.179), channel_id=1, source_target_pairs={{2,0},{4,2},{6,4},{7,6},{5,7},{3,5},{1,3},{0,1},{10,8},{12,10},{14... | collective-permute-start | bytes 884744 | tf_op jit(solution)/shard_map/ppermute | solution.py:323
  (33 other events, 241.0 us)
